TPU v7x, 128 devices: a whole 4x4x4 slice. The times are simulated.
128 devices in a mesh: ctx: 16 (over x, z_hi, core), fsdp: 8 (over y, z_lo).
Axes of the slice: x: 4, y: 4, z: 4 (z_hi: 2, z_lo: 2; z = z_hi * 2 + z_lo), core: 2. Of those that a mesh axis runs over, the one named last changes fastest.
Arguments:
- tokens: bfloat16 [8, 3072, 1024], P('fsdp', 'ctx'), may hold values from -6 to 6
- positions: int32 [8, 3072], P('fsdp', 'ctx'), may hold values from 0 to 3071, as said below
- cotangent: bfloat16 [8, 3072, 1024], P('fsdp', 'ctx'), may hold values from -6 to 6
- attn_gain: bfloat16 [1024], P('fsdp'), may hold values from 0.25 to 1.75
- w_query: bfloat16 [1024, 1024], P('fsdp'), may hold values from -0.1875 to 0.1875
- w_key: bfloat16 [1024, 512], P('fsdp'), may hold values from -0.1875 to 0.1875
- w_value: bfloat16 [1024, 512], P('fsdp'), may hold values from -0.1875 to 0.1875
- query_gain: bfloat16 [64], P('fsdp'), may hold values from 0.25 to 1.75
- key_gain: bfloat16 [64], P('fsdp'), may hold values from 0.25 to 1.75
- w_out: bfloat16 [1024, 1024], P('fsdp'), may hold values from -3 to 3
- ffn_gain: bfloat16 [1024], P('fsdp'), may hold values from 0.25 to 1.75
- w_gate: bfloat16 [1024, 4608], P('fsdp'), may hold values from -0.1875 to 0.1875
- w_up: bfloat16 [1024, 4608], P('fsdp'), may hold values from -0.1875 to 0.1875
- w_down: bfloat16 [4608, 1024], P('fsdp'), may hold values from -0.09375 to 0.09375
Outputs:
- result: bfloat16 [8, 3072, 1024], P('fsdp', 'ctx')
- grad_tokens: bfloat16 [8, 3072, 1024], P('fsdp', 'ctx')
- grad_attn_gain: float32 [1024], P('fsdp')
- grad_w_query: float32 [1024, 1024], P('fsdp')
- grad_w_key: float32 [1024, 512], P('fsdp')
- grad_w_value: float32 [1024, 512], P('fsdp')
- grad_query_gain: float32 [64], P('fsdp')
- grad_key_gain: float32 [64], P('fsdp')
- grad_w_out: float32 [1024, 1024], P('fsdp')
- grad_ffn_gain: float32 [1024], P('fsdp')
- grad_w_gate: float32 [1024, 4608], P('fsdp')
- grad_w_up: float32 [1024, 4608], P('fsdp')
- grad_w_down: float32 [4608, 1024], P('fsdp')
Inputs may be any that keep to these rules, and one draw needn't show every extreme that they name: In each sequence the positions rise by one from token to token, except at one token between a quarter and three quarters of the way through the sequence, where they restart at 0; the token just before the restart has position 3071.
All inputs are finite; a program needn't handle non-finite values.
Results may differ from a plain program's by a relative error of at most 0.028.
Values may be sent and summed in bfloat16 or wider, within the bound.
No kernel may reach another device: no remote copies, remote signals or barrier semaphores. Data moves between devices by JAX's collectives and lax.ppermute only.
A program may use at most 192 MiB of HBM per device.

v0:
```python
import jax
import jax.numpy as jnp
from jax import lax
from jax.sharding import PartitionSpec as P

EPSILON = 1e-05
ROPE_BASE = 1000000.0


def from_behind(block, axis, distance):
    devices = range(lax.axis_size(axis))
    route = [(i - distance, i) for i in devices if i - distance in devices]
    return lax.ppermute(block, axis, route)


def shifted(value, axis, steps):
    count = lax.axis_size(axis)
    pairs = [(source, (source + steps) % count) for source in range(count)]
    return lax.ppermute(value, axis, pairs)


def trans_dot(left, right):
    return lax.dot_general(
        left, right, (((0,), (0,)), ((), ())), preferred_element_type=jnp.float32
    )


def back_dot(left, right):
    return lax.dot_general(
        left, right, (((1,), (1,)), ((), ())), preferred_element_type=jnp.float32
    )


def plain_dot(left, right):
    return jnp.dot(left, right, preferred_element_type=jnp.float32)


def norm_scale(inputs):
    return lax.rsqrt(jnp.mean(inputs * inputs, axis=-1, keepdims=True) + EPSILON)


def norm_back(inputs, scales, gains, grads):
    weighted = grads * gains
    moment = jnp.mean(weighted * inputs, axis=-1, keepdims=True)
    return scales * weighted - inputs * scales * scales * scales * moment


def rotary_tables(token_pos, head_size):
    halves = head_size // 2
    frequency = ROPE_BASE ** (-(jnp.arange(halves, dtype=jnp.float32) * 2.0 / head_size))
    angles = token_pos.astype(jnp.float32)[:, None] * frequency[None, :]
    return (jnp.cos(angles)[:, None, :], jnp.sin(angles)[:, None, :])


def rotate(inputs, cosines, sines):
    halves = inputs.shape[-1] // 2
    former = inputs[..., :halves]
    latter = inputs[..., halves:]
    return jnp.concatenate(
        [former * cosines - latter * sines, latter * cosines + former * sines], axis=-1
    )


def rotate_back(grads, cosines, sines):
    halves = grads.shape[-1] // 2
    former = grads[..., :halves]
    latter = grads[..., halves:]
    return jnp.concatenate(
        [former * cosines + latter * sines, latter * cosines - former * sines], axis=-1
    )


def allowed_keys(owner_idx, block_rows, query_ids, start_ids):
    key_ids = owner_idx * block_rows + jnp.arange(block_rows, dtype=jnp.int32)
    return (key_ids[None, :] <= query_ids[:, None]) & (key_ids[None, :] >= start_ids[:, None])


def local(
    tokens,
    positions,
    cotangent,
    attn_gain,
    w_query,
    w_key,
    w_value,
    query_gain,
    key_gain,
    w_out,
    ffn_gain,
    w_gate,
    w_up,
    w_down,
):
    cycle_size = lax.axis_size("ctx")
    ctx_index = lax.axis_index("ctx")
    block_rows = tokens.shape[1]
    x_float = tokens[0].astype(jnp.float32)
    token_pos = positions[0]
    norm_attn, full_query, full_key, full_value, norm_query, norm_key, full_out = (
        lax.all_gather(attn_gain, "fsdp", axis=0, tiled=True),
        lax.all_gather(w_query, "fsdp", axis=0, tiled=True),
        lax.all_gather(w_key, "fsdp", axis=0, tiled=True),
        lax.all_gather(w_value, "fsdp", axis=0, tiled=True),
        lax.all_gather(query_gain, "fsdp", axis=0, tiled=True),
        lax.all_gather(key_gain, "fsdp", axis=0, tiled=True),
        lax.all_gather(w_out, "fsdp", axis=0, tiled=True),
    )
    head_size = norm_query.shape[0]
    head_count = full_query.shape[1] // head_size
    key_heads = full_key.shape[1] // head_size
    group_size = head_count // key_heads
    scale_attn = norm_scale(x_float)
    gain_first = norm_attn.astype(jnp.float32)
    normed = (x_float * scale_attn * gain_first).astype(jnp.bfloat16)
    query_raw = plain_dot(normed, full_query).reshape(block_rows, head_count, head_size)
    key_raw = plain_dot(normed, full_key).reshape(block_rows, key_heads, head_size)
    value_low = (
        plain_dot(normed, full_value).astype(jnp.bfloat16).reshape(block_rows, key_heads, head_size)
    )
    scale_query = norm_scale(query_raw)
    scale_key = norm_scale(key_raw)
    cosines, sines = rotary_tables(token_pos, head_size)
    query_rot = rotate(
        query_raw * scale_query * norm_query.astype(jnp.float32), cosines, sines
    ).astype(jnp.bfloat16)
    query_rot = query_rot.reshape(block_rows, key_heads, group_size, head_size)
    key_rot = rotate(key_raw * scale_key * norm_key.astype(jnp.float32), cosines, sines).astype(
        jnp.bfloat16
    )
    pair_home = jnp.stack([key_rot, value_low])
    query_ids = ctx_index * block_rows + jnp.arange(block_rows, dtype=jnp.int32)
    start_ids = query_ids - token_pos

    def attend(stats, pair_now, owner_idx):

        def compute(old_stats):
            row_top, row_total, output_sum = old_stats
            allowed = allowed_keys(owner_idx, block_rows, query_ids, start_ids)
            scores = (
                jnp.einsum(
                    "bkgd,lkd->kgbl", query_rot, pair_now[0], preferred_element_type=jnp.float32
                )
                * 0.125
            )
            scores = jnp.where(allowed[None, None], scores, -jnp.inf)
            new_top = jnp.maximum(row_top, jnp.max(scores, axis=-1))
            factor = jnp.exp(row_top - new_top)
            weights = jnp.exp(scores - new_top[..., None])
            row_total = row_total * factor + jnp.sum(weights, axis=-1)
            partial_out = jnp.einsum(
                "kgbl,lkd->bkgd",
                weights.astype(jnp.bfloat16),
                pair_now[1],
                preferred_element_type=jnp.float32,
            )
            output_sum = output_sum * jnp.transpose(factor, (2, 0, 1))[..., None] + partial_out
            return (new_top, row_total, output_sum)

        def skipped(old_stats):
            return old_stats

        return lax.cond(owner_idx <= ctx_index, compute, skipped, stats)

    stored = jnp.zeros((1,), jnp.bfloat16)

    def forward_turn(turn_idx, carry_now):
        pair_now, stats, stored_now = carry_now
        owner_idx = (ctx_index - turn_idx) % cycle_size
        stats = attend(stats, pair_now, owner_idx)
        pair_now = from_behind(pair_now, "ctx", 1)
        return (pair_now, stats, stored_now)

    start_stats = (
        jnp.full((key_heads, group_size, block_rows), -jnp.inf, jnp.float32),
        jnp.zeros((key_heads, group_size, block_rows), jnp.float32),
        jnp.zeros((block_rows, key_heads, group_size, head_size), jnp.float32),
    )
    pair_last, stats, stored = lax.fori_loop(
        0, cycle_size - 1, forward_turn, (pair_home, start_stats, stored)
    )
    last_owner = (ctx_index + 1) % cycle_size
    row_top, row_total, output_sum = attend(stats, pair_last, last_owner)
    log_total = row_top + jnp.log(row_total)
    attn_float = output_sum / jnp.transpose(row_total, (2, 0, 1))[..., None]
    attn_low = attn_float.reshape(block_rows, head_count * head_size).astype(jnp.bfloat16)
    hidden = x_float + plain_dot(attn_low, full_out)
    norm_ffn, full_gate, full_up, full_down = (
        lax.all_gather(ffn_gain, "fsdp", axis=0, tiled=True),
        lax.all_gather(w_gate, "fsdp", axis=0, tiled=True),
        lax.all_gather(w_up, "fsdp", axis=0, tiled=True),
        lax.all_gather(w_down, "fsdp", axis=0, tiled=True),
    )
    scale_ffn = norm_scale(hidden)
    mlp_input = (hidden * scale_ffn * norm_ffn.astype(jnp.float32)).astype(jnp.bfloat16)
    gate_proj = plain_dot(mlp_input, full_gate)
    up_proj = plain_dot(mlp_input, full_up)
    gate_sigmoid = jax.nn.sigmoid(gate_proj)
    mlp_hidden = (gate_proj * gate_sigmoid * up_proj).astype(jnp.bfloat16)
    result = (hidden + plain_dot(mlp_hidden, full_down)).astype(jnp.bfloat16)
    back_ffn = (
        lax.all_gather(ffn_gain, "fsdp", axis=0, tiled=True),
        lax.all_gather(w_gate, "fsdp", axis=0, tiled=True),
        lax.all_gather(w_up, "fsdp", axis=0, tiled=True),
        lax.all_gather(w_down, "fsdp", axis=0, tiled=True),
    )
    grad_output = cotangent[0]
    grad_float = grad_output.astype(jnp.float32)
    grad_mlp = back_dot(grad_output, back_ffn[3])
    grad_gate_low = (
        grad_mlp * up_proj * gate_sigmoid * (1.0 + gate_proj * (1.0 - gate_sigmoid))
    ).astype(jnp.bfloat16)
    grad_up_low = (grad_mlp * gate_proj * gate_sigmoid).astype(jnp.bfloat16)
    grad_mlp_input = back_dot(grad_gate_low, back_ffn[1]) + back_dot(grad_up_low, back_ffn[2])
    grad_ffn_gain = jnp.sum(grad_mlp_input * hidden * scale_ffn, axis=0)
    grad_hidden = grad_float + norm_back(
        hidden, scale_ffn, back_ffn[0].astype(jnp.float32), grad_mlp_input
    )
    grad_down = trans_dot(mlp_hidden, grad_output)
    grad_gate_w = trans_dot(mlp_input, grad_gate_low)
    grad_up_w = trans_dot(mlp_input, grad_up_low)
    sum_ffn_gain, sum_gate, sum_up, sum_down = (
        lax.psum_scatter(
            grad_ffn_gain.astype(jnp.bfloat16), "fsdp", scatter_dimension=0, tiled=True
        ).astype(jnp.float32),
        lax.psum_scatter(
            grad_gate_w.astype(jnp.bfloat16), "fsdp", scatter_dimension=0, tiled=True
        ).astype(jnp.float32),
        lax.psum_scatter(
            grad_up_w.astype(jnp.bfloat16), "fsdp", scatter_dimension=0, tiled=True
        ).astype(jnp.float32),
        lax.psum_scatter(
            grad_down.astype(jnp.bfloat16), "fsdp", scatter_dimension=0, tiled=True
        ).astype(jnp.float32),
    )
    back_attn = (
        lax.all_gather(attn_gain, "fsdp", axis=0, tiled=True),
        lax.all_gather(w_query, "fsdp", axis=0, tiled=True),
        lax.all_gather(w_key, "fsdp", axis=0, tiled=True),
        lax.all_gather(w_value, "fsdp", axis=0, tiled=True),
        lax.all_gather(query_gain, "fsdp", axis=0, tiled=True),
        lax.all_gather(key_gain, "fsdp", axis=0, tiled=True),
        lax.all_gather(w_out, "fsdp", axis=0, tiled=True),
    )
    hidden_low = grad_hidden.astype(jnp.bfloat16)
    grad_attn = (
        back_dot(hidden_low, back_attn[6])
        .astype(jnp.bfloat16)
        .reshape(block_rows, key_heads, group_size, head_size)
    )
    row_delta = jnp.transpose(
        jnp.sum(grad_attn.astype(jnp.float32) * attn_float, axis=-1), (1, 2, 0)
    )

    def attend_back(pair_now, grads_now, owner_idx):

        def compute(old_grads):
            pair_grad, query_grad = old_grads
            allowed = allowed_keys(owner_idx, block_rows, query_ids, start_ids)
            scores = (
                jnp.einsum(
                    "bkgd,lkd->kgbl", query_rot, pair_now[0], preferred_element_type=jnp.float32
                )
                * 0.125
            )
            probs = jnp.exp(jnp.where(allowed[None, None], scores, -jnp.inf) - log_total[..., None])
            prob_grad = jnp.einsum(
                "bkgd,lkd->kgbl", grad_attn, pair_now[1], preferred_element_type=jnp.float32
            )
            score_grad = (probs * (prob_grad - row_delta[..., None])).astype(jnp.bfloat16)
            query_grad = (
                query_grad
                + jnp.einsum(
                    "kgbl,lkd->bkgd", score_grad, pair_now[0], preferred_element_type=jnp.float32
                )
                * 0.125
            )
            key_grad = (
                jnp.einsum(
                    "kgbl,bkgd->lkd", score_grad, query_rot, preferred_element_type=jnp.float32
                )
                * 0.125
            )
            value_grad = jnp.einsum(
                "kgbl,bkgd->lkd",
                probs.astype(jnp.bfloat16),
                grad_attn,
                preferred_element_type=jnp.float32,
            )
            return (pair_grad + jnp.stack([key_grad, value_grad]), query_grad)

        def skipped(old_grads):
            return old_grads

        return lax.cond(owner_idx <= ctx_index, compute, skipped, grads_now)

    def back_step(turn_idx, pair_now, grads_now):
        owner_idx = (ctx_index - turn_idx) % cycle_size
        pair_grad, query_grad = attend_back(pair_now, grads_now, owner_idx)
        pair_grad = shifted(pair_grad.astype(jnp.bfloat16), "ctx", 1).astype(pair_grad.dtype)
        return (pair_grad, query_grad)

    def back_turn(turn_idx, carry_now):
        pair_now, grads_now = carry_now
        grads_now = back_step(turn_idx, pair_now, grads_now)
        pair_now = from_behind(pair_now, "ctx", 1)
        return (pair_now, grads_now)

    start_grads = (
        jnp.zeros((2, block_rows, key_heads, head_size), jnp.float32),
        jnp.zeros((block_rows, key_heads, group_size, head_size), jnp.float32),
    )
    pair_end, grads_now = lax.fori_loop(0, cycle_size - 1, back_turn, (pair_home, start_grads))
    pair_grad, query_grad = back_step(cycle_size - 1, pair_end, grads_now)
    grad_key_rot = rotate_back(pair_grad[0], cosines, sines)
    grad_query_rot = rotate_back(
        query_grad.reshape(block_rows, head_count, head_size), cosines, sines
    )
    grad_query_gain = jnp.sum(grad_query_rot * query_raw * scale_query, axis=(0, 1))
    grad_key_gain = jnp.sum(grad_key_rot * key_raw * scale_key, axis=(0, 1))
    query_back = norm_back(query_raw, scale_query, back_attn[4].astype(jnp.float32), grad_query_rot)
    query_back = query_back.reshape(block_rows, head_count * head_size).astype(jnp.bfloat16)
    key_back = norm_back(key_raw, scale_key, back_attn[5].astype(jnp.float32), grad_key_rot)
    key_back = key_back.reshape(block_rows, key_heads * head_size).astype(jnp.bfloat16)
    value_back = pair_grad[1].reshape(block_rows, key_heads * head_size).astype(jnp.bfloat16)
    grad_normed = (
        back_dot(query_back, back_attn[1])
        + back_dot(key_back, back_attn[2])
        + back_dot(value_back, back_attn[3])
    )
    grad_attn_gain = jnp.sum(grad_normed * x_float * scale_attn, axis=0)
    grad_tokens = (
        grad_hidden + norm_back(x_float, scale_attn, back_attn[0].astype(jnp.float32), grad_normed)
    ).astype(jnp.bfloat16)
    grad_out_w = trans_dot(attn_low, hidden_low)
    grad_query_w = trans_dot(normed, query_back)
    grad_key_w = trans_dot(normed, key_back)
    grad_value_w = trans_dot(normed, value_back)
    sum_attn_gain, sum_query, sum_key, sum_value, sum_query_gain, sum_key_gain, sum_out = (
        lax.psum_scatter(
            grad_attn_gain.astype(jnp.bfloat16), "fsdp", scatter_dimension=0, tiled=True
        ).astype(jnp.float32),
        lax.psum_scatter(
            grad_query_w.astype(jnp.bfloat16), "fsdp", scatter_dimension=0, tiled=True
        ).astype(jnp.float32),
        lax.psum_scatter(
            grad_key_w.astype(jnp.bfloat16), "fsdp", scatter_dimension=0, tiled=True
        ).astype(jnp.float32),
        lax.psum_scatter(
            grad_value_w.astype(jnp.bfloat16), "fsdp", scatter_dimension=0, tiled=True
        ).astype(jnp.float32),
        lax.psum_scatter(
            grad_query_gain.astype(jnp.bfloat16), "fsdp", scatter_dimension=0, tiled=True
        ).astype(jnp.float32),
        lax.psum_scatter(
            grad_key_gain.astype(jnp.bfloat16), "fsdp", scatter_dimension=0, tiled=True
        ).astype(jnp.float32),
        lax.psum_scatter(
            grad_out_w.astype(jnp.bfloat16), "fsdp", scatter_dimension=0, tiled=True
        ).astype(jnp.float32),
    )
    totals = (
        lax.psum(sum_attn_gain.astype(jnp.bfloat16), "ctx").astype(jnp.float32),
        lax.psum(sum_query.astype(jnp.bfloat16), "ctx").astype(jnp.float32),
        lax.psum(sum_key.astype(jnp.bfloat16), "ctx").astype(jnp.float32),
        lax.psum(sum_value.astype(jnp.bfloat16), "ctx").astype(jnp.float32),
        lax.psum(sum_query_gain.astype(jnp.bfloat16), "ctx").astype(jnp.float32),
        lax.psum(sum_key_gain.astype(jnp.bfloat16), "ctx").astype(jnp.float32),
        lax.psum(sum_out.astype(jnp.bfloat16), "ctx").astype(jnp.float32),
        lax.psum(sum_ffn_gain.astype(jnp.bfloat16), "ctx").astype(jnp.float32),
        lax.psum(sum_gate.astype(jnp.bfloat16), "ctx").astype(jnp.float32),
        lax.psum(sum_up.astype(jnp.bfloat16), "ctx").astype(jnp.float32),
        lax.psum(sum_down.astype(jnp.bfloat16), "ctx").astype(jnp.float32),
    )
    return (
        result[None],
        grad_tokens[None],
        totals[0],
        totals[1],
        totals[2],
        totals[3],
        totals[4],
        totals[5],
        totals[6],
        totals[7],
        totals[8],
        totals[9],
        totals[10],
    )


def solution(mesh):
    placed = (
        P("fsdp", "ctx", None),
        P("fsdp", "ctx"),
        P("fsdp", "ctx", None),
        P("fsdp"),
        P("fsdp", None),
        P("fsdp", None),
        P("fsdp", None),
        P("fsdp"),
        P("fsdp"),
        P("fsdp", None),
        P("fsdp"),
        P("fsdp", None),
        P("fsdp", None),
        P("fsdp", None),
    )
    return jax.shard_map(
        local,
        mesh=mesh,
        in_specs=placed,
        out_specs=(
            P("fsdp", "ctx", None),
            P("fsdp", "ctx", None),
            P("fsdp"),
            P("fsdp", None),
            P("fsdp", None),
            P("fsdp", None),
            P("fsdp"),
            P("fsdp"),
            P("fsdp", None),
            P("fsdp"),
            P("fsdp", None),
            P("fsdp", None),
            P("fsdp", None),
        ),
        check_vma=False,
    )
```

profile of v0, /device:TPU:1, one launch (start us, length us, event | category | flops | bytes accessed | tf_op | source)
XLA Modules:
  0.0 2248.3 jit_solution(2971056924112681428)
XLA Ops:
  90.8 52.1 %all-gather.14.cloned.1.call-done = bf16[1024,1024]{1,0:T(8,128)(2,1)} async-done(((bf16[128,1024]{1,0:T(8,128)(2,1)}), bf16[1024,1024]{1,0:T(8,128)(2,1)}) %all-gather.14.cloned.1.call-update) | async-done | bytes 2097168 | tf_op jit(solution)/shard_map/all_gather | solution.py:101
  148.1 497.9 %while.42 = (s32[]{:T(128)}, bf16[2,192,8,64]{1,3,2,0:T(8,128)(2,1)S(1)}, f32[8,2,192]{2,1,0:T(2,128)S(1)}, f32[8,2,192]{2,1,0:T(2,128)S(1)}, f32[192,8,2,64]{0,...) while((s32[]{:T(128)}, ...), condition=%wide.region_8.9_spmd.clone, body=%wide.region_3.8_spmd.clone.sunk | while | flops 157996432 | bytes 12277440 | solution.py:178
  226.1 35.7 %collective-permute-done = bf16[2,192,8,64]{1,3,2,0:T(8,128)(2,1)S(1)} collective-permute-done((bf16[2,192,8,64]{1,3,2,0:T(8,128)(2,1)}, bf16[2,192,8,64]{1,3,2,0:T(8,128)(2,1)S(1)}, u32[]{:S(2)}, u32[]{:S(2)}) %collective-permute-start) | collective-permute-done | bytes 393248 | tf_op jit(solution)/shard_map/while/body/eval_jaxpr/ppermute | solution.py:13
  268.4 27.0 %collective-permute-done = bf16[2,192,8,64]{1,3,2,0:T(8,128)(2,1)S(1)} collective-permute-done((bf16[2,192,8,64]{1,3,2,0:T(8,128)(2,1)}, bf16[2,192,8,64]{1,3,2,0:T(8,128)(2,1)S(1)}, u32[]{:S(2)}, u32[]{:S(2)}) %collective-permute-start) | collective-permute-done | bytes 393248 | tf_op jit(solution)/shard_map/while/body/eval_jaxpr/ppermute | solution.py:13
  302.1 30.2 %collective-permute-done = bf16[2,192,8,64]{1,3,2,0:T(8,128)(2,1)S(1)} collective-permute-done((bf16[2,192,8,64]{1,3,2,0:T(8,128)(2,1)}, bf16[2,192,8,64]{1,3,2,0:T(8,128)(2,1)S(1)}, u32[]{:S(2)}, u32[]{:S(2)}) %collective-permute-start) | collective-permute-done | bytes 393248 | tf_op jit(solution)/shard_map/while/body/eval_jaxpr/ppermute | solution.py:13
  338.9 27.0 %collective-permute-done = bf16[2,192,8,64]{1,3,2,0:T(8,128)(2,1)S(1)} collective-permute-done((bf16[2,192,8,64]{1,3,2,0:T(8,128)(2,1)}, bf16[2,192,8,64]{1,3,2,0:T(8,128)(2,1)S(1)}, u32[]{:S(2)}, u32[]{:S(2)}) %collective-permute-start) | collective-permute-done | bytes 393248 | tf_op jit(solution)/shard_map/while/body/eval_jaxpr/ppermute | solution.py:13
  372.6 30.2 %collective-permute-done = bf16[2,192,8,64]{1,3,2,0:T(8,128)(2,1)S(1)} collective-permute-done((bf16[2,192,8,64]{1,3,2,0:T(8,128)(2,1)}, bf16[2,192,8,64]{1,3,2,0:T(8,128)(2,1)S(1)}, u32[]{:S(2)}, u32[]{:S(2)}) %collective-permute-start) | collective-permute-done | bytes 393248 | tf_op jit(solution)/shard_map/while/body/eval_jaxpr/ppermute | solution.py:13
  409.4 27.0 %collective-permute-done = bf16[2,192,8,64]{1,3,2,0:T(8,128)(2,1)S(1)} collective-permute-done((bf16[2,192,8,64]{1,3,2,0:T(8,128)(2,1)}, bf16[2,192,8,64]{1,3,2,0:T(8,128)(2,1)S(1)}, u32[]{:S(2)}, u32[]{:S(2)}) %collective-permute-start) | collective-permute-done | bytes 393248 | tf_op jit(solution)/shard_map/while/body/eval_jaxpr/ppermute | solution.py:13
  456.1 36.3 %collective-permute-done = bf16[2,192,8,64]{1,3,2,0:T(8,128)(2,1)S(1)} collective-permute-done((bf16[2,192,8,64]{1,3,2,0:T(8,128)(2,1)}, bf16[2,192,8,64]{1,3,2,0:T(8,128)(2,1)S(1)}, u32[]{:S(2)}, u32[]{:S(2)}) %collective-permute-start) | collective-permute-done | bytes 393248 | tf_op jit(solution)/shard_map/while/body/eval_jaxpr/ppermute | solution.py:13
  499.0 30.2 %collective-permute-done = bf16[2,192,8,64]{1,3,2,0:T(8,128)(2,1)S(1)} collective-permute-done((bf16[2,192,8,64]{1,3,2,0:T(8,128)(2,1)}, bf16[2,192,8,64]{1,3,2,0:T(8,128)(2,1)S(1)}, u32[]{:S(2)}, u32[]{:S(2)}) %collective-permute-start) | collective-permute-done | bytes 393248 | tf_op jit(solution)/shard_map/while/body/eval_jaxpr/ppermute | solution.py:13
  535.8 30.2 %collective-permute-done = bf16[2,192,8,64]{1,3,2,0:T(8,128)(2,1)S(1)} collective-permute-done((bf16[2,192,8,64]{1,3,2,0:T(8,128)(2,1)}, bf16[2,192,8,64]{1,3,2,0:T(8,128)(2,1)S(1)}, u32[]{:S(2)}, u32[]{:S(2)}) %collective-permute-start) | collective-permute-done | bytes 393248 | tf_op jit(solution)/shard_map/while/body/eval_jaxpr/ppermute | solution.py:13
  572.7 29.9 %collective-permute-done = bf16[2,192,8,64]{1,3,2,0:T(8,128)(2,1)S(1)} collective-permute-done((bf16[2,192,8,64]{1,3,2,0:T(8,128)(2,1)}, bf16[2,192,8,64]{1,3,2,0:T(8,128)(2,1)S(1)}, u32[]{:S(2)}, u32[]{:S(2)}) %collective-permute-start) | collective-permute-done | bytes 393248 | tf_op jit(solution)/shard_map/while/body/eval_jaxpr/ppermute | solution.py:13
  609.5 36.5 %collective-permute-done = bf16[2,192,8,64]{1,3,2,0:T(8,128)(2,1)S(1)} collective-permute-done((bf16[2,192,8,64]{1,3,2,0:T(8,128)(2,1)}, bf16[2,192,8,64]{1,3,2,0:T(8,128)(2,1)S(1)}, u32[]{:S(2)}, u32[]{:S(2)}) %collective-permute-start) | collective-permute-done | bytes 393248 | tf_op jit(solution)/shard_map/while/body/eval_jaxpr/ppermute | solution.py:13
  670.2 180.7 %all-gather.22.cloned.1.call-done = bf16[4608,1024]{1,0:T(8,128)(2,1)} async-done(((bf16[576,1024]{1,0:T(8,128)(2,1)}), bf16[4608,1024]{1,0:T(8,128)(2,1)}) %all-gather.22.cloned.1.call-update) | async-done | bytes 9437200 | tf_op jit(solution)/shard_map/all_gather | solution.py:191
  880.9 371.7 %while.43 = (s32[]{:T(128)}, bf16[2,192,8,64]{1,3,2,0:T(8,128)(2,1)S(1)}, f32[2,192,8,64]{1,3,2,0:T(8,128)}, f32[192,8,2,64]{0,3,2,1:T(8,128)S(1)}, s32[]{:T(128...) while((s32[]{:T(128)}, ...), condition=%wide.region_19.20_spmd.clone, body=%wide.region_16.19_spmd.clone.sunk | while | flops 384971136 | bytes 36844400 | solution.py:312
  1313.7 28.7 %reduce-scatter.10.cloned.1.call-done = bf16[128,512]{1,0:T(8,128)(2,1)} async-done(((bf16[1024,512]{1,0:T(8,128)(2,1)}), bf16[128,512]{1,0:T(8,128)(2,1)}) %reduce-scatter.10.cloned.1.call-update) | async-done | bytes 131088 | tf_op jit(solution)/shard_map/reduce_scatter | solution.py:345
  1342.4 40.8 %reduce-scatter.12.cloned.1.call-done = bf16[128,512]{1,0:T(8,128)(2,1)} async-done(((bf16[1024,512]{1,0:T(8,128)(2,1)}), bf16[128,512]{1,0:T(8,128)(2,1)}) %reduce-scatter.12.cloned.1.call-update) | async-done | bytes 131088 | tf_op jit(solution)/shard_map/reduce_scatter | solution.py:348
  1383.2 56.6 %reduce-scatter.8.cloned.1.call-done = bf16[128,1024]{1,0:T(8,128)(2,1)} async-done(((bf16[1024,1024]{1,0:T(8,128)(2,1)}), bf16[128,1024]{1,0:T(8,128)(2,1)}) %reduce-scatter.8.cloned.1.call-update) | async-done | bytes 262160 | tf_op jit(solution)/shard_map/reduce_scatter | solution.py:342
  1439.8 55.3 %reduce-scatter.14.cloned.1.call-done = bf16[128,1024]{1,0:T(8,128)(2,1)} async-done(((bf16[1024,1024]{1,0:T(8,128)(2,1)}), bf16[128,1024]{1,0:T(8,128)(2,1)}) %reduce-scatter.14.cloned.1.call-update) | async-done | bytes 262160 | tf_op jit(solution)/shard_map/reduce_scatter | solution.py:357
  1495.1 193.3 %reduce-scatter.16.cloned.1.call-done = bf16[128,4608]{1,0:T(8,128)(2,1)} async-done(((bf16[1024,4608]{1,0:T(8,128)(2,1)}), bf16[128,4608]{1,0:T(8,128)(2,1)}) %reduce-scatter.16.cloned.1.call-update) | async-done | bytes 1179664 | tf_op jit(solution)/shard_map/reduce_scatter | solution.py:225
  1688.4 192.3 %reduce-scatter.18.cloned.1.call-done = bf16[128,4608]{1,0:T(8,128)(2,1)} async-done(((bf16[1024,4608]{1,0:T(8,128)(2,1)}), bf16[128,4608]{1,0:T(8,128)(2,1)}) %reduce-scatter.18.cloned.1.call-update) | async-done | bytes 1179664 | tf_op jit(solution)/shard_map/reduce_scatter | solution.py:228
  1880.7 192.2 %reduce-scatter.20.cloned.1.call-done = bf16[576,1024]{1,0:T(8,128)(2,1)} async-done(((bf16[4608,1024]{1,0:T(8,128)(2,1)}), bf16[576,1024]{1,0:T(8,128)(2,1)}) %reduce-scatter.20.cloned.1.call-update) | async-done | bytes 1179664 | tf_op jit(solution)/shard_map/reduce_scatter | solution.py:231
  2101.8 36.4 %all-reduce.6 = (bf16[128]{0:T(256)(128)(2,1)S(1)}, bf16[8]{0:T(256)(128)(2,1)S(1)}, bf16[8]{0:T(256)(128)(2,1)S(1)}, bf16[128]{0:T(256)(128)(2,1)S(1)}) all-reduce(bf16[128]{0:T(256)(128)(2,1)S(1)} %dynamic-slice.3, bf16[8]{0:T(256)(128)(2,1)S(1)} %dynamic-slice.5, ...), channel_id=1, replica_groups=mesh['ctx'=16,'fsdp'=8] {'ctx'}, use_global_device_ids=true, to_apply=%region_27.28 | all-reduce | flops 272 | bytes 1088 | tf_op jit(solution)/shard_map/psum | solution.py:362
  2141.3 88.3 %all-reduce.12.cloned.1.call-done = (bf16[128,1024]{1,0:T(8,128)(2,1)}, bf16[128,512]{1,0:T(8,128)(2,1)}, bf16[128,512]{1,0:T(8,128)(2,1)}, bf16[128,1024]{1,0:T...) async-done(((bf16[128,1024]{1,0:T(8,128)(2,1)}, bf16[128,512]{1,0:T(8,128)(2,1)}, bf16[128,512]{1,0:T(8,128)(2,1)}, ...) | async-done | bytes 4325392 | tf_op jit(solution)/shard_map/psum | solution.py:363
  (571 shorter events, 799.1 us)
Async XLA Ops:
  7.3 52.1 %all-gather.12.cloned.1.call-start = ((), (), s32[]{:S(2)}) async-start(), calls=%async_computation.8 | async-start | bytes 1179648 | tf_op jit(solution)/shard_map/all_gather | solution.py:103
  8.0 79.8 %all-gather.10.cloned.1.call-start = ((), (), s32[]{:S(2)}) async-start(), calls=%async_computation.7 | async-start | bytes 1179648 | tf_op jit(solution)/shard_map/all_gather | solution.py:102
  8.7 134.2 %all-gather.14.cloned.1.call-start = ((), (), s32[]{:S(2)}) async-start(), calls=%async_computation.9 | async-start | bytes 2359296 | tf_op jit(solution)/shard_map/all_gather | solution.py:101
  9.5 637.1 %all-gather.16.cloned.1.call-start = ((), (), s32[]{:S(2)}) async-start(), calls=%async_computation.10 | async-start | bytes 2359296 | tf_op jit(solution)/shard_map/all_gather | solution.py:106
  10.0 639.9 %all-gather.18.cloned.1.call-start = ((), (), s32[]{:S(2)}) async-start(), calls=%async_computation.11 | async-start | bytes 10616832 | tf_op jit(solution)/shard_map/all_gather | solution.py:189
  10.6 652.1 %all-gather.20.cloned.1.call-start = ((), (), s32[]{:S(2)}) async-start(), calls=%async_computation.12 | async-start | bytes 10616832 | tf_op jit(solution)/shard_map/all_gather | solution.py:190
  11.2 839.6 %all-gather.22.cloned.1.call-start = ((), (), s32[]{:S(2)}) async-start(), calls=%async_computation.13 | async-start | bytes 10616832 | tf_op jit(solution)/shard_map/all_gather | solution.py:191
  12.0 1330.4 %reduce-scatter.10.cloned.1.call-start = ((), (), s32[]{:S(2)}) async-start(), calls=%async_computation.15 | async-start | bytes 1179648 | tf_op jit(solution)/shard_map/reduce_scatter | solution.py:345
  148.9 34.4 %collective-permute-start = (bf16[2,192,8,64]{1,3,2,0:T(8,128)(2,1)}, bf16[2,192,8,64]{1,3,2,0:T(8,128)(2,1)S(1)}, u32[]{:S(2)}, u32[]{:S(2)}) collective-permute-start(bf16[2,192,8,64]{1,3,2,0:T(8,128)(2,1)} %copy.103), channel_id=1, source_target_pairs={{0,8},{8,16},{16,24},{24,32},{32,40},{40,48},{48,56},{56,64},{64,7... | collective-permute-start | bytes 1179656 | tf_op jit(solution)/shard_map/while/body/eval_jaxpr/ppermute | solution.py:13
  220.2 41.6 %collective-permute-start = (bf16[2,192,8,64]{1,3,2,0:T(8,128)(2,1)}, bf16[2,192,8,64]{1,3,2,0:T(8,128)(2,1)S(1)}, u32[]{:S(2)}, u32[]{:S(2)}) collective-permute-start(bf16[2,192,8,64]{1,3,2,0:T(8,128)(2,1)} %copy.103), channel_id=1, source_target_pairs={{0,8},{8,16},{16,24},{24,32},{32,40},{40,48},{48,56},{56,64},{64,7... | collective-permute-start | bytes 1179656 | tf_op jit(solution)/shard_map/while/body/eval_jaxpr/ppermute | solution.py:13
  296.3 36.0 %collective-permute-start = (bf16[2,192,8,64]{1,3,2,0:T(8,128)(2,1)}, bf16[2,192,8,64]{1,3,2,0:T(8,128)(2,1)S(1)}, u32[]{:S(2)}, u32[]{:S(2)}) collective-permute-start(bf16[2,192,8,64]{1,3,2,0:T(8,128)(2,1)} %copy.103), channel_id=1, source_target_pairs={{0,8},{8,16},{16,24},{24,32},{32,40},{40,48},{48,56},{56,64},{64,7... | collective-permute-start | bytes 1179656 | tf_op jit(solution)/shard_map/while/body/eval_jaxpr/ppermute | solution.py:13
  366.8 36.0 %collective-permute-start = (bf16[2,192,8,64]{1,3,2,0:T(8,128)(2,1)}, bf16[2,192,8,64]{1,3,2,0:T(8,128)(2,1)S(1)}, u32[]{:S(2)}, u32[]{:S(2)}) collective-permute-start(bf16[2,192,8,64]{1,3,2,0:T(8,128)(2,1)} %copy.103), channel_id=1, source_target_pairs={{0,8},{8,16},{16,24},{24,32},{32,40},{40,48},{48,56},{56,64},{64,7... | collective-permute-start | bytes 1179656 | tf_op jit(solution)/shard_map/while/body/eval_jaxpr/ppermute | solution.py:13
  450.3 42.1 %collective-permute-start = (bf16[2,192,8,64]{1,3,2,0:T(8,128)(2,1)}, bf16[2,192,8,64]{1,3,2,0:T(8,128)(2,1)S(1)}, u32[]{:S(2)}, u32[]{:S(2)}) collective-permute-start(bf16[2,192,8,64]{1,3,2,0:T(8,128)(2,1)} %copy.103), channel_id=1, source_target_pairs={{0,8},{8,16},{16,24},{24,32},{32,40},{40,48},{48,56},{56,64},{64,7... | collective-permute-start | bytes 1179656 | tf_op jit(solution)/shard_map/while/body/eval_jaxpr/ppermute | solution.py:13
  493.2 36.0 %collective-permute-start = (bf16[2,192,8,64]{1,3,2,0:T(8,128)(2,1)}, bf16[2,192,8,64]{1,3,2,0:T(8,128)(2,1)S(1)}, u32[]{:S(2)}, u32[]{:S(2)}) collective-permute-start(bf16[2,192,8,64]{1,3,2,0:T(8,128)(2,1)} %copy.103), channel_id=1, source_target_pairs={{0,8},{8,16},{16,24},{24,32},{32,40},{40,48},{48,56},{56,64},{64,7... | collective-permute-start | bytes 1179656 | tf_op jit(solution)/shard_map/while/body/eval_jaxpr/ppermute | solution.py:13
  530.0 36.0 %collective-permute-start = (bf16[2,192,8,64]{1,3,2,0:T(8,128)(2,1)}, bf16[2,192,8,64]{1,3,2,0:T(8,128)(2,1)S(1)}, u32[]{:S(2)}, u32[]{:S(2)}) collective-permute-start(bf16[2,192,8,64]{1,3,2,0:T(8,128)(2,1)} %copy.103), channel_id=1, source_target_pairs={{0,8},{8,16},{16,24},{24,32},{32,40},{40,48},{48,56},{56,64},{64,7... | collective-permute-start | bytes 1179656 | tf_op jit(solution)/shard_map/while/body/eval_jaxpr/ppermute | solution.py:13
  566.8 35.7 %collective-permute-start = (bf16[2,192,8,64]{1,3,2,0:T(8,128)(2,1)}, bf16[2,192,8,64]{1,3,2,0:T(8,128)(2,1)S(1)}, u32[]{:S(2)}, u32[]{:S(2)}) collective-permute-start(bf16[2,192,8,64]{1,3,2,0:T(8,128)(2,1)} %copy.103), channel_id=1, source_target_pairs={{0,8},{8,16},{16,24},{24,32},{32,40},{40,48},{48,56},{56,64},{64,7... | collective-permute-start | bytes 1179656 | tf_op jit(solution)/shard_map/while/body/eval_jaxpr/ppermute | solution.py:13
  603.4 42.7 %collective-permute-start = (bf16[2,192,8,64]{1,3,2,0:T(8,128)(2,1)}, bf16[2,192,8,64]{1,3,2,0:T(8,128)(2,1)S(1)}, u32[]{:S(2)}, u32[]{:S(2)}) collective-permute-start(bf16[2,192,8,64]{1,3,2,0:T(8,128)(2,1)} %copy.103), channel_id=1, source_target_pairs={{0,8},{8,16},{16,24},{24,32},{32,40},{40,48},{48,56},{56,64},{64,7... | collective-permute-start | bytes 1179656 | tf_op jit(solution)/shard_map/while/body/eval_jaxpr/ppermute | solution.py:13
  1281.9 101.3 %reduce-scatter.12.cloned.1.call-start = ((), (), s32[]{:S(2)}) async-start(), calls=%async_computation.16 | async-start | bytes 1179648 | tf_op jit(solution)/shard_map/reduce_scatter | solution.py:348
  1284.6 155.2 %reduce-scatter.8.cloned.1.call-start = ((), (), s32[]{:S(2)}) async-start(), calls=%async_computation.14 | async-start | bytes 2359296 | tf_op jit(solution)/shard_map/reduce_scatter | solution.py:342
  1290.4 204.7 %reduce-scatter.14.cloned.1.call-start = ((), (), s32[]{:S(2)}) async-start(), calls=%async_computation.17 | async-start | bytes 2359296 | tf_op jit(solution)/shard_map/reduce_scatter | solution.py:357
  1292.5 395.8 %reduce-scatter.16.cloned.1.call-start = ((), (), s32[]{:S(2)}) async-start(), calls=%async_computation.18 | async-start | bytes 10616832 | tf_op jit(solution)/shard_map/reduce_scatter | solution.py:225
  1299.1 581.6 %reduce-scatter.18.cloned.1.call-start = ((), (), s32[]{:S(2)}) async-start(), calls=%async_computation.19 | async-start | bytes 10616832 | tf_op jit(solution)/shard_map/reduce_scatter | solution.py:228
  1305.7 767.2 %reduce-scatter.20.cloned.1.call-start = ((), (), s32[]{:S(2)}) async-start(), calls=%async_computation.20 | async-start | bytes 10616832 | tf_op jit(solution)/shard_map/reduce_scatter | solution.py:231
  1313.4 916.2 %all-reduce.12.cloned.1.call-start = ((), (), s32[]{:S(2)}) async-start(), calls=%async_computation.21 | async-start | bytes 8650752 | tf_op jit(solution)/shard_map/psum | solution.py:363
  (133 other events, 3094.6 us)
Sparse Core Ops, SparseCore 0:
  9.7 37.8 all-gather.11
  49.3 38.4 all-gather.9
  89.4 53.4 all-gather.13
  144.4 60.3 all-gather.15
  206.3 233.2 all-gather.17
  441.1 221.5 all-gather.19
  664.4 186.4 all-gather.21
  1282.0 60.2 reduce-scatter.9
  1344.8 38.3 reduce-scatter.11
  1386.0 53.7 reduce-scatter.7
  1442.8 52.2 reduce-scatter.13
  1497.4 190.9 reduce-scatter.15
  1690.8 189.8 reduce-scatter.17
  1883.0 189.8 reduce-scatter.19
  2075.8 153.6 all-reduce.11
where the time goes:
time: 2260 us; the launch traced here: 2250 us
  waiting for transfers between devices  1660 us (73%)
  starting transfers between devices  259 us (11%)
  matrix products  107 us (5%)
  blocking collectives  96.1 us (4%)
  other arithmetic  77 us (3%)
  local copies, waits for them, and re-layouts  26.9 us (1%)
    ppermute x30, waiting for transfers between devices, from_behind(): return lax.ppermute(block, axis, route)  436 us
    ppermute x30, starting transfers between devices, from_behind(): return lax.ppermute(block, axis, route)  196 us
    reduce_scatter x1, waiting for transfers between devices, local(): lax.psum_scatter(grad_gate_w.astype(jnp.bfloat16), 'fsdp', scatter_dimens...  193 us
    reduce_scatter x1, waiting for transfers between devices, local(): lax.psum_scatter(grad_up_w.astype(jnp.bfloat16), 'fsdp', scatter_dimensio...  192 us
    reduce_scatter x1, waiting for transfers between devices, local(): lax.psum_scatter(grad_down.astype(jnp.bfloat16), 'fsdp', scatter_dimensio...  192 us
    all_gather x1, waiting for transfers between devices, local(): lax.all_gather(w_down, 'fsdp', axis=0, tiled=True)  181 us
    ppermute x16, waiting for transfers between devices, shifted(): return lax.ppermute(value, axis, pairs)  109 us
    psum x1, waiting for transfers between devices, local(): lax.psum(sum_query.astype(jnp.bfloat16), 'ctx').astype(jnp.float32)  88.3 us
  transfers between devices with their start and end apart: 61, of which 46 were waited for; matrix products, arithmetic and copies ran while one was open for 5% of the time, Pallas kernels for 0%

commit v1 on v0

v1 whole, which is shorter than its diff:
```python
import functools

import jax
import jax.numpy as jnp
from jax import lax
from jax.experimental import pallas as pl
from jax.experimental.pallas import tpu as pltpu
from jax.sharding import PartitionSpec as P

EPSILON = 1e-05
ROPE_BASE = 1000000.0
F32 = jnp.float32
BF16 = jnp.bfloat16
LOG2E = 1.4426950408889634
SCALE = 0.125


def move_ctx(v, dx=0, dz=0, dc=0):
    pairs = [
        (a * 4 + b * 2 + c, ((a + dx) % 4) * 4 + (b ^ dz) * 2 + (c ^ dc))
        for a in range(4)
        for b in range(2)
        for c in range(2)
    ]
    return lax.ppermute(v, "ctx", pairs)


def move_fsdp(v, dy=0, dz=0):
    pairs = [
        (a * 2 + b, ((a + dy) % 4) * 2 + (b ^ dz)) for a in range(4) for b in range(2)
    ]
    return lax.ppermute(v, "fsdp", pairs)


def swap_roles(v):
    pairs = []
    for t in range(8):
        for h in range(2):
            for f in range(8):
                src = ((t // 2) * 4 + h * 2 + t % 2) * 8 + f
                dst = ((f // 2) * 4 + h * 2 + f % 2) * 8 + t
                pairs.append((src, dst))
    return lax.ppermute(v, ("ctx", "fsdp"), pairs)


def gather_group(u):
    one, two, three = move_ctx(u, dx=1), move_ctx(u, dx=2), move_ctx(u, dx=3)
    return [[v, move_ctx(v, dc=1)] for v in (u, one, two, three)]


def joined(blocks):
    return jnp.concatenate([b for pair in blocks for b in pair], axis=0)


def scatter_group(part):
    other = move_ctx(part[1:, 1].astype(BF16), dc=1)
    other_home = move_ctx(part[0, 1].astype(BF16), dc=1)
    total = part[0, 0].astype(F32) + other_home.astype(F32)
    for r in (1, 2, 3):
        acc = part[r, 0].astype(F32) + other[r - 1].astype(F32)
        total = total + move_ctx(acc.astype(BF16), dx=-r).astype(F32)
    return total


def exchange_group(blocks):
    other = move_ctx(jnp.stack([blocks[r][1] for r in range(4)]), dc=1)
    out = [[blocks[0][0], other[0]]]
    for r in (1, 2, 3):
        both = move_ctx(jnp.stack([blocks[r][0], other[r]]), dx=-r)
        out.append([both[0], both[1]])
    return out


def gather_fsdp(u, y, zl):
    o = move_fsdp(u, dz=1)
    low = zl == 0
    pair = jnp.stack([jnp.where(low, u, o), jnp.where(low, o, u)])
    full = jnp.zeros((4,) + pair.shape, u.dtype)
    for d in range(4):
        got = pair if d == 0 else move_fsdp(pair, dy=d)
        full = lax.dynamic_update_index_in_dim(full, got, (y - d) % 4, 0)
    return full.reshape((8,) + u.shape)


def scatter_fsdp(part, y, zl):
    part = part.reshape((4, 2) + part.shape[1:])
    give = lax.dynamic_index_in_dim(part, 1 - zl, 1, keepdims=False).astype(BF16)
    keep = lax.dynamic_index_in_dim(part, zl, 1, keepdims=False)
    acc = keep.astype(F32) + move_fsdp(give, dz=1).astype(F32)
    total = lax.dynamic_index_in_dim(acc, y, 0, keepdims=False)
    low = acc.astype(BF16)
    for d in (1, 2, 3):
        give = lax.dynamic_index_in_dim(low, (y + d) % 4, 0, keepdims=False)
        total = total + move_fsdp(give, dy=d).astype(F32)
    return total


def rounded(v):
    return lax.reduce_precision(v, 8, 7)


def sum_z(v):
    mine = rounded(v)
    other = move_ctx(mine.astype(BF16), dz=1)
    return rounded(mine + other.astype(F32)).astype(BF16)


def trans_dot(left, right):
    return lax.dot_general(
        left, right, (((0,), (0,)), ((), ())), preferred_element_type=F32
    )


def back_dot(left, right):
    return lax.dot_general(
        left, right, (((1,), (1,)), ((), ())), preferred_element_type=F32
    )


def plain_dot(left, right):
    return jnp.dot(left, right, preferred_element_type=F32)


def norm_scale(inputs):
    return lax.rsqrt(jnp.mean(inputs * inputs, axis=-1, keepdims=True) + EPSILON)


def norm_back(inputs, scales, gains, grads):
    weighted = grads * gains
    moment = jnp.mean(weighted * inputs, axis=-1, keepdims=True)
    return scales * weighted - inputs * scales * scales * scales * moment


def slot_of(j, x, zh):
    return (x - j // 2) % 4 + 4 * jnp.where(j % 2 == zh, 0, 1)


def attend_kernel(meta, q_ref, k_ref, v_ref, qs_ref, kid_ref, o_ref, ob_ref, l_ref):
    r = pl.program_id(0)
    x, zh = meta[0], meta[1]
    rows = q_ref.shape[2]
    q = q_ref[...].reshape(2 * rows, q_ref.shape[3])
    last = 2 * ((x - r) % 4) + zh
    qid = qs_ref[0, :, 0:1]
    start = qs_ref[0, :, 1:2]

    def step(j, acc):
        slot = slot_of(j, x, zh)
        s = back_dot(q, k_ref[slot])
        kid = kid_ref[slot]
        allowed = (kid <= qid) & (kid >= start)
        w = jnp.exp2(s * (SCALE * LOG2E)).reshape(2, rows, s.shape[1])
        w = jnp.where(allowed[None], w, 0.0).reshape(s.shape)
        return acc + plain_dot(w.astype(BF16), v_ref[slot])

    acc = lax.fori_loop(
        meta[2 + r], last + 1, step, jnp.zeros((2 * rows, v_ref.shape[2]), F32)
    )
    o = acc[:, :64] / acc[:, 64:65]
    o = jnp.concatenate([o[:rows], o[rows:]], axis=1)
    o_ref[0] = o
    ob_ref[0] = o.astype(BF16)
    l_ref[0] = acc.T[64:65]


def attend(meta, q, k, vx, qs, kid):
    rows = q.shape[2]
    full = lambda a: pl.BlockSpec(a.shape, lambda r, m: (0,) * a.ndim)
    return pl.pallas_call(
        attend_kernel,
        grid_spec=pltpu.PrefetchScalarGridSpec(
            num_scalar_prefetch=1,
            grid=(4,),
            in_specs=[
                pl.BlockSpec((2, 1, rows, 64), lambda r, m: (0, r, 0, 0)),
                full(k),
                full(vx),
                pl.BlockSpec((1, rows, 2), lambda r, m: (r, 0, 0)),
                full(kid),
            ],
            out_specs=[
                pl.BlockSpec((1, rows, 128), lambda r, m: (r, 0, 0)),
                pl.BlockSpec((1, rows, 128), lambda r, m: (r, 0, 0)),
                pl.BlockSpec((1, 1, 2 * rows), lambda r, m: (r, 0, 0)),
            ],
        ),
        out_shape=[
            jax.ShapeDtypeStruct((4, rows, 128), F32),
            jax.ShapeDtypeStruct((4, rows, 128), BF16),
            jax.ShapeDtypeStruct((4, 1, 2 * rows), F32),
        ],
        cost_estimate=pl.CostEstimate(
            flops=4_000_000_000, bytes_accessed=6_000_000, transcendentals=6_000_000
        ),
        name="attend",
    )(meta, q, k, vx, qs, kid)


def attend_back_kernel(
    meta, q_ref, do_ref, k_ref, v_ref, lse_ref, delta_ref, qs_ref, kid_ref,
    dq_ref, dk_ref, dv_ref,
):
    r = pl.program_id(0)
    x, zh = meta[0], meta[1]
    rows = q_ref.shape[2]
    q = q_ref[...].reshape(2 * rows, q_ref.shape[3])
    do = do_ref[0]
    do = jnp.concatenate([do[:, :64], do[:, 64:]], axis=0)
    last = 2 * ((x - r) % 4) + zh
    qid = qs_ref[0, 0:1]
    start = qs_ref[0, 1:2]
    lse = lse_ref[0]
    delta = delta_ref[0]

    @pl.when(r == 0)
    def _():
        dk_ref[...] = jnp.zeros_like(dk_ref)
        dv_ref[...] = jnp.zeros_like(dv_ref)

    def step(j, dq):
        slot = slot_of(j, x, zh)
        k = k_ref[slot]
        s = back_dot(k, q)
        kid = kid_ref[slot]
        allowed = (kid <= qid) & (kid >= start)
        p = jnp.where(allowed, jnp.exp2(s * (SCALE * LOG2E) - lse), 0.0)
        dp = back_dot(v_ref[slot], do)
        ds = (p * (dp - delta)).astype(BF16)
        dk_ref[slot] += plain_dot(ds, q)
        dv_ref[slot] += plain_dot(p.astype(BF16), do)
        return dq + trans_dot(ds, k)

    dq = lax.fori_loop(
        meta[2 + r], last + 1, step, jnp.zeros((2 * rows, 64), F32)
    )
    dq_ref[...] = (dq * SCALE).reshape(dq_ref.shape)


def attend_back(meta, q, do, k, v, lse, delta, qs, kid):
    rows = q.shape[2]
    full = lambda a: pl.BlockSpec(a.shape, lambda r, m: (0,) * a.ndim)
    row = lambda n: pl.BlockSpec((1, n, 2 * rows), lambda r, m: (r, 0, 0))
    return pl.pallas_call(
        attend_back_kernel,
        grid_spec=pltpu.PrefetchScalarGridSpec(
            num_scalar_prefetch=1,
            grid=(4,),
            in_specs=[
                pl.BlockSpec((2, 1, rows, 64), lambda r, m: (0, r, 0, 0)),
                pl.BlockSpec((1, rows, 128), lambda r, m: (r, 0, 0)),
                full(k),
                full(v),
                row(1),
                row(1),
                row(2),
                full(kid),
            ],
            out_specs=[
                pl.BlockSpec((2, 1, rows, 64), lambda r, m: (0, r, 0, 0)),
                pl.BlockSpec(k.shape, lambda r, m: (0, 0, 0)),
                pl.BlockSpec(k.shape, lambda r, m: (0, 0, 0)),
            ],
        ),
        out_shape=[
            jax.ShapeDtypeStruct(q.shape, F32),
            jax.ShapeDtypeStruct(k.shape, F32),
            jax.ShapeDtypeStruct(k.shape, F32),
        ],
        cost_estimate=pl.CostEstimate(
            flops=10_000_000_000, bytes_accessed=9_000_000, transcendentals=6_000_000
        ),
        name="attend_back",
    )(meta, q, do, k, v, lse, delta, qs, kid)


def local(
    tokens, positions, cotangent, attn_gain, w_query, w_key, w_value, query_gain,
    key_gain, w_out, ffn_gain, w_gate, w_up, w_down,
):
    ctx, fsdp = lax.axis_index("ctx"), lax.axis_index("fsdp")
    x, zh, c = ctx // 4, (ctx // 2) % 2, ctx % 2
    t = x * 2 + c
    y, zl = fsdp // 2, fsdp % 2
    first = c == 0
    rows = tokens.shape[1]
    width = tokens.shape[2]
    part_rows = w_query.shape[0]
    hidden_all = w_gate.shape[1]
    hid = hidden_all // 8
    toks = 8 * rows

    def half(w, size):
        both = lax.dynamic_slice_in_dim(w, x * (2 * size), 2 * size, 1)
        return jnp.where(first, both[:, :size], both[:, size:])

    pos = positions[0]
    pos_rows = jnp.stack([pos // 64, pos % 64]).astype(F32).astype(BF16)
    pos_rows = jnp.pad(pos_rows, ((0, 14), (0, width - rows)))
    packed = jnp.concatenate([tokens[0], pos_rows], axis=0)
    blocks = gather_group(packed)
    gains = jnp.concatenate([attn_gain, ffn_gain])[None]
    small = jnp.concatenate([query_gain, key_gain, jnp.zeros((240,), BF16)])[None]
    piece = jnp.concatenate(
        [
            jnp.concatenate([half(w_query, 128), half(w_key, 64), half(w_value, 64)], axis=1),
            gains,
            small,
            jnp.zeros((14, 256), BF16),
        ],
        axis=0,
    )
    got = gather_fsdp(piece, y, zl)
    w_qkv = got[:, :part_rows].reshape(width, 256)
    norm_attn = got[:, part_rows, :part_rows].reshape(width).astype(F32)
    norm_ffn = got[:, part_rows, part_rows:].reshape(width).astype(F32)
    norm_query = got[:, part_rows + 1, :8].reshape(64).astype(F32)
    norm_key = got[:, part_rows + 1, 8:16].reshape(64).astype(F32)
    out_cols = gather_fsdp(half(w_out, 128), y, zl).reshape(width, 128)
    full_out = jnp.zeros((width, width), BF16)
    for r, pair in enumerate(gather_group(out_cols)):
        both = jnp.concatenate(
            [jnp.where(first, pair[0], pair[1]), jnp.where(first, pair[1], pair[0])], axis=1
        )
        full_out = lax.dynamic_update_slice_in_dim(full_out, both, ((x - r) % 4) * 256, 1)
    gate_up = jnp.concatenate([half(w_gate, hid), half(w_up, hid)], axis=1)
    gate_up = gather_fsdp(gate_up, y, zl).reshape(width, 2 * hid)
    w_gate_t, w_up_t = gate_up[:, :hid], gate_up[:, hid:]
    down_rows = hid // 8
    down = swap_roles(lax.dynamic_slice_in_dim(w_down, t * down_rows, down_rows, 0))
    w_down_t = gather_fsdp(down, y, zl).reshape(hid, width)
    grad_output = joined(gather_group(cotangent[0]))

    x_all = jnp.concatenate([b[:rows] for pair in blocks for b in pair], axis=0)
    pos_hi = jnp.concatenate([b[rows, :rows] for pair in blocks for b in pair])
    pos_lo = jnp.concatenate([b[rows + 1, :rows] for pair in blocks for b in pair])
    token_pos = (pos_hi.astype(F32) * 64.0 + pos_lo.astype(F32)).astype(jnp.int32)
    x_float = x_all.astype(F32)
    normed = (x_float * norm_scale(x_float) * norm_attn).astype(BF16)
    qkv = plain_dot(normed, w_qkv)
    raw = jnp.stack([qkv[:, 0:64], qkv[:, 64:128], qkv[:, 128:192]])
    value_low = qkv[:, 192:].astype(BF16)
    scale_raw = norm_scale(raw)
    gain_raw = jnp.stack([norm_query, norm_query, norm_key])[:, None, :]
    frequency = ROPE_BASE ** (-(jnp.arange(32, dtype=F32) * 2.0 / 64))
    angles = token_pos.astype(F32)[:, None] * frequency[None, :]
    cosines, sines = jnp.cos(angles), jnp.sin(angles)
    cos_all = jnp.concatenate([cosines, cosines], axis=1)
    sin_all = jnp.concatenate([sines, sines], axis=1)
    normal = raw * scale_raw * gain_raw
    turned = jnp.concatenate([-normal[..., 32:], normal[..., :32]], axis=-1)
    rot = (normal * cos_all + turned * sin_all).astype(BF16)
    query_rot = rot[:2].reshape(2, 4, 2 * rows, 64)
    pair_home = jnp.concatenate([rot[2], value_low], axis=1)
    pair_away = move_ctx(pair_home, dz=1)
    pairs = jnp.concatenate([pair_home, pair_away]).reshape(8, 2 * rows, 128)
    keys = pairs[..., :64]
    values = pairs[..., 64:]
    values_one = jnp.concatenate(
        [values, jnp.ones((8, 2 * rows, 1), BF16), jnp.zeros((8, 2 * rows, 63), BF16)], axis=-1
    )
    chips = (x - jnp.arange(4, dtype=jnp.int32)) % 4
    cores = jnp.stack([c, 1 - c]).astype(jnp.int32)
    base = (chips * 4)[:, None] + cores[None, :]
    inner = jnp.arange(rows, dtype=jnp.int32)
    ids = lambda z: ((base + 2 * z)[:, :, None] * rows + inner).reshape(4, 2 * rows)
    query_ids = ids(zh)
    key_ids = jnp.concatenate([query_ids, ids(1 - zh)])
    start_ids = query_ids - token_pos.reshape(4, 2 * rows)
    lowest = jnp.maximum(jnp.min(start_ids, axis=1), 0) // (2 * rows)
    meta = jnp.concatenate([jnp.stack([x, zh]), lowest]).astype(jnp.int32)
    attn_float, attn_part, row_total = attend(
        meta,
        query_rot,
        keys,
        values_one,
        jnp.stack([query_ids, start_ids], axis=-1),
        key_ids[:, None, :],
    )

    part4 = attn_part.reshape(4, 2, rows, 128)
    arrived = exchange_group([[part4[r, 0], part4[r, 1]] for r in range(4)])
    attn_low = jnp.zeros((rows, width), BF16)
    for r in range(4):
        own, oth = arrived[r]
        both = jnp.concatenate([jnp.where(first, own, oth), jnp.where(first, oth, own)], axis=1)
        attn_low = lax.dynamic_update_slice_in_dim(attn_low, both, ((x + r) % 4) * 256, 1)
    x_own = tokens[0].astype(F32)
    hidden = x_own + plain_dot(attn_low, full_out)
    scale_ffn = norm_scale(hidden)
    mlp_own = (hidden * scale_ffn * norm_ffn).astype(BF16)

    mlp_input = joined(gather_group(mlp_own))
    gate_proj = plain_dot(mlp_input, w_gate_t)
    up_proj = plain_dot(mlp_input, w_up_t)
    grad_mlp = back_dot(grad_output, w_down_t)
    gate_sigmoid = jax.nn.sigmoid(gate_proj)
    mlp_hidden = (gate_proj * gate_sigmoid * up_proj).astype(BF16)
    grad_gate_low = (
        grad_mlp * up_proj * gate_sigmoid * (1.0 + gate_proj * (1.0 - gate_sigmoid))
    ).astype(BF16)
    grad_up_low = (grad_mlp * gate_proj * gate_sigmoid).astype(BF16)
    grad_in_part = back_dot(grad_gate_low, w_gate_t) + back_dot(grad_up_low, w_up_t)
    split = lambda v: v.reshape((4, 2, rows) + v.shape[1:])
    grad_mlp_input = scatter_group(split(grad_in_part.astype(BF16)))
    grad_hidden = cotangent[0].astype(F32) + norm_back(
        hidden, scale_ffn, norm_ffn, grad_mlp_input
    )
    hidden_low = grad_hidden.astype(BF16)
    grad_attn_own = back_dot(hidden_low, full_out).astype(BF16)

    def head_block(r, s):
        pair = lax.dynamic_slice_in_dim(grad_attn_own, ((x - r) % 4) * 256, 256, 1)
        swap = first if s == 0 else jnp.logical_not(first)
        return jnp.where(swap, pair[:, :128], pair[:, 128:])

    arrived = exchange_group([[head_block(r, s) for s in range(2)] for r in range(4)])
    grad_attn = joined([arrived[(4 - r) % 4] for r in range(4)]).reshape(4, 2 * rows, 128)
    delta = grad_attn.astype(F32) * attn_float
    row_delta = jnp.stack(
        [jnp.sum(delta[..., :64], axis=-1), jnp.sum(delta[..., 64:], axis=-1)], axis=1
    ).reshape(4, 1, 4 * rows)
    twice = lambda v: jnp.concatenate([v, v], axis=-1)
    grad_query, grad_key, grad_value = attend_back(
        meta,
        query_rot,
        grad_attn,
        keys,
        values,
        jnp.log2(row_total),
        row_delta,
        jnp.stack([twice(query_ids), twice(start_ids)], axis=1),
        key_ids[:, :, None],
    )
    pair_grad = jnp.concatenate([grad_key * SCALE, grad_value], axis=-1)
    away = move_ctx(pair_grad[4:].astype(BF16), dz=1)
    pair_grad = (pair_grad[:4] + away.astype(F32)).reshape(toks, 128)
    grad_rot = jnp.concatenate([grad_query.reshape(2, toks, 64), pair_grad[None, :, :64]])
    turned = jnp.concatenate([grad_rot[..., 32:], -grad_rot[..., :32]], axis=-1)
    grad_normal = grad_rot * cos_all + turned * sin_all
    gain_sums = jnp.sum(grad_normal * raw * scale_raw, axis=1)
    raw_back = norm_back(raw, scale_raw, gain_raw, grad_normal).astype(BF16)
    qkv_back = jnp.concatenate(
        [raw_back[0], raw_back[1], raw_back[2], pair_grad[:, 64:].astype(BF16)], axis=1
    )
    grad_normed = scatter_group(split(back_dot(qkv_back, w_qkv).astype(BF16)))
    scale_own = norm_scale(x_own)
    grad_tokens = (
        grad_hidden + norm_back(x_own, scale_own, norm_attn, grad_normed)
    ).astype(BF16)

    result = scatter_group(split(plain_dot(mlp_hidden, w_down_t).astype(BF16)))
    result = (hidden + result).astype(BF16)

    grad_down = trans_dot(mlp_hidden, grad_output)
    grad_gate_w = trans_dot(mlp_input, grad_gate_low)
    grad_up_w = trans_dot(mlp_input, grad_up_low)
    sum_ffn_gain = (
        jnp.sum(grad_gate_w * w_gate_t.astype(F32), axis=1)
        + jnp.sum(grad_up_w * w_up_t.astype(F32), axis=1)
    ) / norm_ffn
    grad_gu = jnp.concatenate([grad_gate_w.astype(BF16), grad_up_w.astype(BF16)], axis=1)
    piece_gu = sum_z(scatter_fsdp(grad_gu.reshape(8, part_rows, 2 * hid), y, zl))
    piece_down = sum_z(scatter_fsdp(grad_down.astype(BF16).reshape(8, down_rows, width), y, zl))
    piece_down = swap_roles(piece_down)

    grad_out_w = trans_dot(attn_low, hidden_low).astype(BF16)

    def out_block(r, s):
        pair = lax.dynamic_slice_in_dim(grad_out_w, ((x - r) % 4) * 256, 256, 1)
        swap = first if s == 0 else jnp.logical_not(first)
        return jnp.where(swap, pair[:, :128], pair[:, 128:])

    grad_out_t = scatter_group(
        jnp.stack([jnp.stack([out_block(r, s) for s in range(2)]) for r in range(4)])
    )
    piece_out = sum_z(scatter_fsdp(grad_out_t.astype(BF16).reshape(8, part_rows, 128), y, zl))

    grad_qkv_w = trans_dot(normed, qkv_back)
    sum_attn_gain = jnp.sum(grad_qkv_w * w_qkv.astype(F32), axis=1) / norm_attn
    gain_rows = jnp.concatenate(
        [sum_attn_gain.reshape(8, 1, part_rows), sum_ffn_gain.reshape(8, 1, part_rows)], axis=2
    )
    small_rows = jnp.concatenate(
        [
            (gain_sums[0] + gain_sums[1]).reshape(8, 1, 8),
            gain_sums[2].reshape(8, 1, 8),
            jnp.zeros((8, 1, 240), F32),
        ],
        axis=2,
    )
    piece_qkv = jnp.concatenate(
        [
            grad_qkv_w.reshape(8, part_rows, 256),
            gain_rows,
            small_rows,
            jnp.zeros((8, 14, 256), F32),
        ],
        axis=1,
    )
    piece_qkv = sum_z(scatter_fsdp(piece_qkv.astype(BF16), y, zl))

    def in_order(piece):
        for r, (own, oth) in enumerate(gather_group(piece)):
            yield r, jnp.where(first, own, oth), jnp.where(first, oth, own)

    def columns(pieces, size):
        full = jnp.zeros((part_rows, 8 * size), F32)
        for r, one, two in pieces:
            both = jnp.concatenate([one, two], axis=1).astype(F32)
            full = lax.dynamic_update_slice_in_dim(full, both, ((x - r) % 4) * (2 * size), 1)
        return full

    gu = list(in_order(piece_gu))
    total_gate = columns([(r, a[:, :hid], b[:, :hid]) for r, a, b in gu], hid)
    total_up = columns([(r, a[:, hid:], b[:, hid:]) for r, a, b in gu], hid)
    total_down = jnp.zeros(w_down.shape, F32)
    for r, a, b in in_order(piece_down):
        total_down = lax.dynamic_update_slice_in_dim(
            total_down,
            jnp.concatenate([a, b]).astype(F32),
            ((x - r) % 4) * (2 * down_rows),
            0,
        )
    total_out = columns(in_order(piece_out), 128)
    qkv_pieces = list(in_order(piece_qkv))
    rows_of = slice(0, part_rows)
    total_query = columns([(r, a[rows_of, :128], b[rows_of, :128]) for r, a, b in qkv_pieces], 128)
    total_key = columns([(r, a[rows_of, 128:192], b[rows_of, 128:192]) for r, a, b in qkv_pieces], 64)
    total_value = columns([(r, a[rows_of, 192:], b[rows_of, 192:]) for r, a, b in qkv_pieces], 64)
    extra = jnp.zeros((8, 2, 256), F32)
    for r, a, b in qkv_pieces:
        both = jnp.stack([a[part_rows : part_rows + 2], b[part_rows : part_rows + 2]]).astype(F32)
        extra = lax.dynamic_update_slice_in_dim(extra, both, ((x - r) % 4) * 2, 0)
    extra = jnp.sum(extra, axis=0)
    return (
        result[None],
        grad_tokens[None],
        extra[0, :part_rows],
        total_query,
        total_key,
        total_value,
        extra[1, :8],
        extra[1, 8:16],
        total_out,
        extra[0, part_rows:],
        total_gate,
        total_up,
        total_down,
    )


def solution(mesh):
    tok, vec, mat = P("fsdp", "ctx", None), P("fsdp"), P("fsdp", None)
    return jax.shard_map(
        local,
        mesh=mesh,
        in_specs=(
            tok, P("fsdp", "ctx"), tok, vec, mat, mat, mat, vec, vec, mat, vec, mat, mat, mat,
        ),
        out_specs=(tok, tok, vec, mat, mat, mat, vec, vec, mat, vec, mat, mat, mat),
        check_vma=False,
    )
```

time: 2260 us -> 630 us (0.28)
  waiting for transfers between devices: 1660 us -> 174 us
  local copies, waits for them, and re-layouts: 26.9 us -> 123 us
  blocking collectives: 96.1 us -> 0 us
  starting transfers between devices: 259 us -> 172 us
  matrix products: 107 us -> 33.5 us
  Pallas kernels: 0 us -> 30.1 us
    reduce_scatter x7 -> x0, waiting for transfers between devices: 759 us -> none  [the longest x1 193 us: local(): lax.psum_scatter(grad_gate_w.astype(jnp.bfloat16), 'fsdp', scatter_dimens...]
    ppermute x46 -> x124, waiting for transfers between devices: 545 us -> 174 us  [the longest x90 125 us: move_ctx(): return lax.ppermute(v, 'ctx', pairs)]
    all_gather x7 -> x0, waiting for transfers between devices: 265 us -> none  [the longest x1 181 us: local(): lax.all_gather(w_down, 'fsdp', axis=0, tiled=True)]
    psum x1 -> x0, waiting for transfers between devices: 88.3 us -> none  [local(): lax.psum(sum_query.astype(jnp.bfloat16), 'ctx').astype(jnp.float32)]
    ppermute x46 -> x124, starting transfers between devices: 258 us -> 172 us  [the longest x90 112 us: move_ctx(): return lax.ppermute(v, 'ctx', pairs)]
    dot_general x21 -> x5, matrix products: 51.3 us -> 11 us  [plain_dot(): return jnp.dot(left, right, preferred_element_type=F32)]
    psum x1 -> x0, blocking collectives: 36.4 us -> none  [local(): lax.psum(sum_attn_gain.astype(jnp.bfloat16), 'ctx').astype(jnp.float32)]
    all_gather x2 -> x0, blocking collectives: 30.3 us -> none  [the longest x1 16.4 us: local(): lax.all_gather(attn_gain, 'fsdp', axis=0, tiled=True)]
  transfers between devices with their start and end apart: 61 -> 124, of which waited for: 46 -> 43; matrix products, arithmetic and copies ran while one was open for 5% -> 33% of each run, Pallas kernels for 0% -> 5%
where the time goes in v1:
time: 630 us; the launch traced here: 618 us
  waiting for transfers between devices  174 us (28%)
  starting transfers between devices  172 us (27%)
  local copies, waits for them, and re-layouts  123 us (20%)
  other arithmetic  83.1 us (13%)
  matrix products  33.5 us (5%)
  Pallas kernels  30.1 us (5%)
    ppermute x90, waiting for transfers between devices, move_ctx(): return lax.ppermute(v, 'ctx', pairs)  125 us
    ppermute x90, starting transfers between devices, move_ctx(): return lax.ppermute(v, 'ctx', pairs)  112 us
    ppermute x32, starting transfers between devices, move_fsdp(): return lax.ppermute(v, 'fsdp', pairs)  46 us
    ppermute x32, waiting for transfers between devices, move_fsdp(): return lax.ppermute(v, 'fsdp', pairs)  45.5 us
    unnamed x186, local copies, waits for them, and re-layouts  33.7 us
    pallas_call x1, Pallas kernels, attend_back(): pl.pallas_call(attend_back_kernel, grid_spec=pltpu.PrefetchScalarGridSpec...  18.4 us
    ppermute x2, starting transfers between devices, swap_roles(): return lax.ppermute(v, ('ctx', 'fsdp'), pairs)  14 us
    dot_general x5, matrix products, back_dot(): lax.dot_general(left, right, (((1,), (1,)), ((), ())), preferred_element_...  13.3 us
  transfers between devices with their start and end apart: 124, of which 43 were waited for; matrix products, arithmetic and copies ran while one was open for 33% of the time, Pallas kernels for 5%

profile of v1, /device:TPU:1, one launch (start us, length us, event | category | flops | bytes accessed | tf_op | source)
XLA Modules:
  0.0 618.3 jit_solution(6799847873518196495)
XLA Ops:
  40.9 4.9 collective-permute-done.8
  46.5 5.7 collective-permute-done.9
  56.5 9.6 %collective-permute-start.38 = (bf16[72,1024]{1,0:T(8,128)(2,1)S(1)}, bf16[72,1024]{1,0:T(8,128)(2,1)S(1)}, u32[]{:S(2)}, u32[]{:S(2)}) collective-permute-start(bf16[72,1024]{1,0:T(8,128)(2,1)S(1)} %constant_dynamic-slice_fusion.2), channel_id=1, source_target_pairs={{0,0},{1,8},{2,32},{3,40},{4,64},{5,72},{6,96},{7,104},{16,16},{17... | collective-permute-start | bytes 442376 | tf_op jit(solution)/shard_map/ppermute | solution.py:43
  84.4 6.2 collective-permute-start.5
  91.6 7.1 %collective-permute-done.49 = bf16[192,1024]{1,0:T(8,128)(2,1)S(1)} collective-permute-done((bf16[192,1024]{1,0:T(8,128)(2,1)}, bf16[192,1024]{1,0:T(8,128)(2,1)S(1)}, u32[]{:S(2)}, u32[]{:S(2)}) %collective-permute-start.49) | collective-permute-done | bytes 393248 | tf_op jit(solution)/shard_map/ppermute | solution.py:25
  108.2 4.9 collective-permute-start.41
  171.2 5.8 collective-permute-done.11
  185.9 11.7 %attend.1 = (f32[4,384,128]{2,1,0:T(8,128)}, bf16[4,384,128]{2,1,0:T(8,128)(2,1)}, f32[4,1,768]{2,1,0:T(1,128)}) custom-call(s32[6]{0:T(128)} %pad_add_fusion.5.meta, bf16[2,4,384,64]{3,2,1,0:T(8,128)(2,1)} %bitcast.562, bf16[8,384,64]{2,1,0:T(8,128)(2,1)} %get-tuple-element.108.k_ref, bf16[8,384,128]{2,1,0:T(8,128)(2,1)} %maximum_maximum_fusion.v_ref, ...), custom_call_target="tpu_custom_call" | custom-call | flops 4000000000 | bytes 6000000 | tf_op jit(solution)/shard_map/attend/pallas_call | solution.py:169
  243.4 6.9 %collective-permute-done.32 = bf16[192,1024]{1,0:T(8,128)(2,1)} collective-permute-done((bf16[192,1024]{1,0:T(8,128)(2,1)}, bf16[192,1024]{1,0:T(8,128)(2,1)}, u32[]{:S(2)}, u32[]{:S(2)}) %collective-permute-start.32) | collective-permute-done | bytes 393248 | tf_op jit(solution)/shard_map/ppermute | solution.py:25
  292.9 5.7 reshape_reshape.22
  307.5 5.9 constant_dynamic-slice_fusion.1
  313.4 6.2 %copy.92 = bf16[4,1,128,1152]{3,2,0,1:T(8,128)(2,1)} copy(bf16[4,1,128,1152]{2,1,0,3:T(2,128)(2,1)} %get-tuple-element.79) | data formatting | bytes 2359296
  329.8 4.9 copy.91
  334.7 17.2 %collective-permute-done.115 = bf16[72,1024]{1,0:T(8,128)(2,1)} collective-permute-done((bf16[72,1024]{1,0:T(8,128)(2,1)}, bf16[72,1024]{1,0:T(8,128)(2,1)}, u32[]{:S(2)}, u32[]{:S(2)}) %collective-permute-start.115) | collective-permute-done | bytes 147488 | tf_op jit(solution)/shard_map/ppermute | solution.py:25
  369.2 8.3 %collective-permute-start.120 = (bf16[72,1024]{1,0:T(8,128)(2,1)S(1)}, bf16[72,1024]{1,0:T(8,128)(2,1)S(1)}, u32[]{:S(2)}, u32[]{:S(2)}) collective-permute-start(bf16[72,1024]{1,0:T(8,128)(2,1)S(1)} %collective-permute-done.116), channel_id=1, source_target_pairs={{0,64},{8,72},{16,80},{24,88},{32,96},{40,104},{48,112},{56,120},{... | collective-permute-start | bytes 442376 | tf_op jit(solution)/shard_map/ppermute | solution.py:25
  393.0 7.3 %collective-permute-done.102 = bf16[128,1152]{1,0:T(8,128)(2,1)S(1)} collective-permute-done((bf16[128,1152]{1,0:T(8,128)(2,1)S(1)}, bf16[128,1152]{1,0:T(8,128)(2,1)S(1)}, u32[]{:S(2)}, u32[]{:S(2)}) %collective-permute-start.102) | collective-permute-done | bytes 294944 | tf_op jit(solution)/shard_map/ppermute | solution.py:32
  406.7 12.7 %collective-permute-done.59 = bf16[192,1024]{1,0:T(8,128)(2,1)S(1)} collective-permute-done((bf16[192,1024]{1,0:T(8,128)(2,1)S(1)}, bf16[192,1024]{1,0:T(8,128)(2,1)S(1)}, u32[]{:S(2)}, u32[]{:S(2)}) %collective-permute-start.59) | collective-permute-done | bytes 393248 | tf_op jit(solution)/shard_map/ppermute | solution.py:25
  423.7 13.0 %collective-permute-done.47 = bf16[192,1024]{1,0:T(8,128)(2,1)S(1)} collective-permute-done((bf16[192,1024]{1,0:T(8,128)(2,1)S(1)}, bf16[192,1024]{1,0:T(8,128)(2,1)S(1)}, u32[]{:S(2)}, u32[]{:S(2)}) %collective-permute-start.47) | collective-permute-done | bytes 393248 | tf_op jit(solution)/shard_map/ppermute | solution.py:25
  451.5 14.5 %collective-permute-done.61 = bf16[2,192,128]{2,1,0:T(8,128)(2,1)S(1)} collective-permute-done((bf16[2,192,128]{2,1,0:T(8,128)(2,1)S(1)}, bf16[2,192,128]{2,1,0:T(8,128)(2,1)S(1)}, u32[]{:S(2)}, u32[]{:S(2)}) %collective-permute-start.61) | collective-permute-done | bytes 98336 | tf_op jit(solution)/shard_map/ppermute | solution.py:25
  466.2 4.8 collective-permute-done.62
  478.4 18.4 %attend_back.1 = (f32[2,4,384,64]{3,2,1,0:T(8,128)}, f32[8,384,64]{2,1,0:T(8,128)}, f32[8,384,64]{2,1,0:T(8,128)}) custom-call(s32[6]{0:T(128)} %pad_add_fusion.5.meta, bf16[2,4,384,64]{3,2,1,0:T(8,128)(2,1)} %bitcast.563, bf16[4,384,128]{2,1,0:T(8,128)(2,1)} %bitcast.568, bf16[8,384,64]{2,1,0:T(8,128)(2,1)} %get-tuple-element.108.k_ref, ...), custom_call_target="tpu_custom_call" | custom-call | flops 10000000000 | bytes 9000000 | tf_op jit(solution)/shard_map/attend_back/pallas_call | solution.py:243
  545.3 4.9 collective-permute-start.73
  597.4 8.0 %collective-permute-done.69 = bf16[192,1024]{1,0:T(8,128)(2,1)S(1)} collective-permute-done((bf16[192,1024]{1,0:T(8,128)(2,1)S(1)}, bf16[192,1024]{1,0:T(8,128)(2,1)S(1)}, u32[]{:S(2)}, u32[]{:S(2)}) %collective-permute-start.69) | collective-permute-done | bytes 393248 | tf_op jit(solution)/shard_map/ppermute | solution.py:25
  605.5 8.5 %collective-permute-done.68 = bf16[192,1024]{1,0:T(8,128)(2,1)S(1)} collective-permute-done((bf16[192,1024]{1,0:T(8,128)(2,1)S(1)}, bf16[192,1024]{1,0:T(8,128)(2,1)S(1)}, u32[]{:S(2)}, u32[]{:S(2)}) %collective-permute-start.68) | collective-permute-done | bytes 393248 | tf_op jit(solution)/shard_map/ppermute | solution.py:25
  (751 shorter events, 411.7 us)
Async XLA Ops:
  3.3 97.0 %collective-permute-start = (bf16[208,1024]{1,0:T(8,128)(2,1)}, bf16[208,1024]{1,0:T(8,128)(2,1)}, u32[]{:S(2)}, u32[]{:S(2)}) collective-permute-start(bf16[208,1024]{1,0:T(8,128)(2,1)} %fusion.66), channel_id=1, source_target_pairs={{0,8},{8,0},{16,24},{24,16},{32,40},{40,32},{48,56},{56,48},{64,72... | collective-permute-start | bytes 1277960 | tf_op jit(solution)/shard_map/ppermute | solution.py:25
  4.7 97.3 %collective-permute-start.1 = (bf16[208,1024]{1,0:T(8,128)(2,1)}, bf16[208,1024]{1,0:T(8,128)(2,1)}, u32[]{:S(2)}, u32[]{:S(2)}) collective-permute-start(bf16[208,1024]{1,0:T(8,128)(2,1)} %fusion.66), channel_id=1, source_target_pairs={{0,32},{8,40},{16,48},{24,56},{32,64},{40,72},{48,80},{56,88},{64,... | collective-permute-start | bytes 1277960 | tf_op jit(solution)/shard_map/ppermute | solution.py:25
  6.0 98.4 %collective-permute-start.3 = (bf16[208,1024]{1,0:T(8,128)(2,1)}, bf16[208,1024]{1,0:T(8,128)(2,1)}, u32[]{:S(2)}, u32[]{:S(2)}) collective-permute-start(bf16[208,1024]{1,0:T(8,128)(2,1)} %fusion.66), channel_id=1, source_target_pairs={{0,64},{8,72},{16,80},{24,88},{32,96},{40,104},{48,112},{56,120},{... | collective-permute-start | bytes 1277960 | tf_op jit(solution)/shard_map/ppermute | solution.py:25
  25.7 43.2 %collective-permute-start.34 = (bf16[128,1152]{1,0:T(8,128)(2,1)S(1)}, bf16[128,1152]{1,0:T(8,128)(2,1)S(1)}, u32[]{:S(2)}, u32[]{:S(2)}) collective-permute-start(bf16[128,1152]{1,0:T(8,128)(2,1)S(1)} %pad_maximum_fusion.12), channel_id=1, source_target_pairs={{0,1},{1,0},{2,3},{3,2},{4,5},{5,4},{6,7},{7,6},{8,9},{9,8},{10,11... | collective-permute-start | bytes 884744 | tf_op jit(solution)/shard_map/ppermute | solution.py:32
  98.7 33.1 %collective-permute-start.51 = (bf16[192,1024]{1,0:T(8,128)(2,1)}, bf16[192,1024]{1,0:T(8,128)(2,1)S(1)}, u32[]{:S(2)}, u32[]{:S(2)}) collective-permute-start(bf16[192,1024]{1,0:T(8,128)(2,1)} %bitcast.68), channel_id=1, source_target_pairs={{0,64},{8,72},{16,80},{24,88},{32,96},{40,104},{48,112},{56,120},{... | collective-permute-start | bytes 1179656 | tf_op jit(solution)/shard_map/ppermute | solution.py:25
  127.0 92.4 %collective-permute-start.35 = (bf16[2,128,1152]{2,1,0:T(8,128)(2,1)}, bf16[2,128,1152]{2,1,0:T(8,128)(2,1)}, u32[]{:S(2)}, u32[]{:S(2)}) collective-permute-start(bf16[2,128,1152]{2,1,0:T(8,128)(2,1)} %get-tuple-element.125), channel_id=1, source_target_pairs={{0,2},{1,3},{2,4},{3,5},{4,6},{5,7},{6,0},{7,1},{8,10},{9,11},{10,... | collective-permute-start | bytes 1769480 | tf_op jit(solution)/shard_map/ppermute | solution.py:32
  128.1 94.2 %collective-permute-start.36 = (bf16[2,128,1152]{2,1,0:T(8,128)(2,1)}, bf16[2,128,1152]{2,1,0:T(8,128)(2,1)}, u32[]{:S(2)}, u32[]{:S(2)}) collective-permute-start(bf16[2,128,1152]{2,1,0:T(8,128)(2,1)} %get-tuple-element.125), channel_id=1, source_target_pairs={{0,4},{1,5},{2,6},{3,7},{4,0},{5,1},{6,2},{7,3},{8,12},{9,13},{10,... | collective-permute-start | bytes 1769480 | tf_op jit(solution)/shard_map/ppermute | solution.py:32
  137.1 96.8 %collective-permute-start.37 = (bf16[2,128,1152]{2,1,0:T(8,128)(2,1)}, bf16[2,128,1152]{2,1,0:T(8,128)(2,1)}, u32[]{:S(2)}, u32[]{:S(2)}) collective-permute-start(bf16[2,128,1152]{2,1,0:T(8,128)(2,1)} %get-tuple-element.125), channel_id=1, source_target_pairs={{0,6},{1,7},{2,0},{3,1},{4,2},{5,3},{6,4},{7,5},{8,14},{9,15},{10,... | collective-permute-start | bytes 1769480 | tf_op jit(solution)/shard_map/ppermute | solution.py:32
  216.3 25.2 %collective-permute-start.28 = (bf16[192,1024]{1,0:T(8,128)(2,1)}, bf16[192,1024]{1,0:T(8,128)(2,1)}, u32[]{:S(2)}, u32[]{:S(2)}) collective-permute-start(bf16[192,1024]{1,0:T(8,128)(2,1)} %get-tuple-element.59), channel_id=1, source_target_pairs={{0,32},{8,40},{16,48},{24,56},{32,64},{40,72},{48,80},{56,88},{64,... | collective-permute-start | bytes 1179656 | tf_op jit(solution)/shard_map/ppermute | solution.py:25
  285.0 75.5 %collective-permute-start.56 = (bf16[3,192,1024]{2,1,0:T(8,128)(2,1)}, bf16[3,192,1024]{2,1,0:T(8,128)(2,1)}, u32[]{:S(2)}, u32[]{:S(2)}) collective-permute-start(bf16[3,192,1024]{2,1,0:T(8,128)(2,1)} %slice_bitcast_fusion.1), channel_id=1, source_target_pairs={{0,8},{8,0},{16,24},{24,16},{32,40},{40,32},{48,56},{56,48},{64,72... | collective-permute-start | bytes 3538952 | tf_op jit(solution)/shard_map/ppermute | solution.py:25
  286.2 76.8 %collective-permute-start.44 = (bf16[3,192,1024]{2,1,0:T(8,128)(2,1)}, bf16[3,192,1024]{2,1,0:T(8,128)(2,1)}, u32[]{:S(2)}, u32[]{:S(2)}) collective-permute-start(bf16[3,192,1024]{2,1,0:T(8,128)(2,1)} %slice_bitcast_fusion.2), channel_id=1, source_target_pairs={{0,8},{8,0},{16,24},{24,16},{32,40},{40,32},{48,56},{56,48},{64,72... | collective-permute-start | bytes 3538952 | tf_op jit(solution)/shard_map/ppermute | solution.py:25
  319.6 49.6 %collective-permute-start.99 = (bf16[4,128,1152]{2,1,0:T(8,128)(2,1)}, bf16[4,128,1152]{2,1,0:T(8,128)(2,1)}, u32[]{:S(2)}, u32[]{:S(2)}) collective-permute-start(bf16[4,128,1152]{2,1,0:T(8,128)(2,1)} %bitcast.551), channel_id=1, source_target_pairs={{0,1},{1,0},{2,3},{3,2},{4,5},{5,4},{6,7},{7,6},{8,9},{9,8},{10,11... | collective-permute-start | bytes 3538952 | tf_op jit(solution)/shard_map/ppermute | solution.py:32
  322.5 29.4 %collective-permute-start.115 = (bf16[72,1024]{1,0:T(8,128)(2,1)}, bf16[72,1024]{1,0:T(8,128)(2,1)}, u32[]{:S(2)}, u32[]{:S(2)}) collective-permute-start(bf16[72,1024]{1,0:T(8,128)(2,1)} %fusion.94), channel_id=1, source_target_pairs={{0,16},{8,24},{16,0},{24,8},{32,48},{40,56},{48,32},{56,40},{64,80... | collective-permute-start | bytes 442376 | tf_op jit(solution)/shard_map/ppermute | solution.py:25
  327.8 77.4 %collective-permute-start.55 = (bf16[192,1024]{1,0:T(8,128)(2,1)}, bf16[192,1024]{1,0:T(8,128)(2,1)}, u32[]{:S(2)}, u32[]{:S(2)}) collective-permute-start(bf16[192,1024]{1,0:T(8,128)(2,1)} %slice_bitcast_fusion.17), channel_id=1, source_target_pairs={{0,8},{8,0},{16,24},{24,16},{32,40},{40,32},{48,56},{56,48},{64,72... | collective-permute-start | bytes 1179656 | tf_op jit(solution)/shard_map/ppermute | solution.py:25
  360.5 63.3 %collective-permute-start.43 = (bf16[192,1024]{1,0:T(8,128)(2,1)S(1)}, bf16[192,1024]{1,0:T(8,128)(2,1)S(1)}, u32[]{:S(2)}, u32[]{:S(2)}) collective-permute-start(bf16[192,1024]{1,0:T(8,128)(2,1)S(1)} %slice_bitcast_fusion.25), channel_id=1, source_target_pairs={{0,8},{8,0},{16,24},{24,16},{32,40},{40,32},{48,56},{56,48},{64,72... | collective-permute-start | bytes 1179656 | tf_op jit(solution)/shard_map/ppermute | solution.py:25
  405.2 31.5 %collective-permute-start.47 = (bf16[192,1024]{1,0:T(8,128)(2,1)S(1)}, bf16[192,1024]{1,0:T(8,128)(2,1)S(1)}, u32[]{:S(2)}, u32[]{:S(2)}) collective-permute-start(bf16[192,1024]{1,0:T(8,128)(2,1)S(1)} %get-tuple-element.74), channel_id=1, source_target_pairs={{0,32},{8,40},{16,48},{24,56},{32,64},{40,72},{48,80},{56,88},{64,... | collective-permute-start | bytes 1179656 | tf_op jit(solution)/shard_map/ppermute | solution.py:25
  421.6 25.5 %collective-permute-start.103 = (bf16[128,1152]{1,0:T(8,128)(2,1)S(1)}, bf16[128,1152]{1,0:T(8,128)(2,1)S(1)}, u32[]{:S(2)}, u32[]{:S(2)}) collective-permute-start(bf16[128,1152]{1,0:T(8,128)(2,1)S(1)} %fusion.95), channel_id=1, source_target_pairs={{0,16},{8,24},{16,0},{24,8},{32,48},{40,56},{48,32},{56,40},{64,80... | collective-permute-start | bytes 884744 | tf_op jit(solution)/shard_map/ppermute | solution.py:25
  446.0 85.1 %collective-permute-start.83 = (bf16[3,1024,128]{2,1,0:T(8,128)(2,1)}, bf16[3,1024,128]{2,1,0:T(8,128)(2,1)}, u32[]{:S(2)}, u32[]{:S(2)}) collective-permute-start(bf16[3,1024,128]{2,1,0:T(8,128)(2,1)} %fusion.29), channel_id=1, source_target_pairs={{0,8},{8,0},{16,24},{24,16},{32,40},{40,32},{48,56},{56,48},{64,72... | collective-permute-start | bytes 2359304 | tf_op jit(solution)/shard_map/ppermute | solution.py:25
  447.3 53.5 %collective-permute-start.104 = (bf16[128,1152]{1,0:T(8,128)(2,1)S(1)}, bf16[128,1152]{1,0:T(8,128)(2,1)}, u32[]{:S(2)}, u32[]{:S(2)}) collective-permute-start(bf16[128,1152]{1,0:T(8,128)(2,1)S(1)} %reduce-precision_convert_fusion), channel_id=1, source_target_pairs={{0,8},{8,0},{16,24},{24,16},{32,40},{40,32},{48,56},{56,48},{64,72... | collective-permute-start | bytes 884744 | tf_op jit(solution)/shard_map/ppermute | solution.py:25
  447.8 60.4 %collective-permute-start.105 = (bf16[128,1152]{1,0:T(8,128)(2,1)S(1)}, bf16[128,1152]{1,0:T(8,128)(2,1)}, u32[]{:S(2)}, u32[]{:S(2)}) collective-permute-start(bf16[128,1152]{1,0:T(8,128)(2,1)S(1)} %reduce-precision_convert_fusion), channel_id=1, source_target_pairs={{0,32},{8,40},{16,48},{24,56},{32,64},{40,72},{48,80},{56,88},{64,... | collective-permute-start | bytes 884744 | tf_op jit(solution)/shard_map/ppermute | solution.py:25
  447.8 64.1 %collective-permute-start.107 = (bf16[128,1152]{1,0:T(8,128)(2,1)S(1)}, bf16[128,1152]{1,0:T(8,128)(2,1)}, u32[]{:S(2)}, u32[]{:S(2)}) collective-permute-start(bf16[128,1152]{1,0:T(8,128)(2,1)S(1)} %reduce-precision_convert_fusion), channel_id=1, source_target_pairs={{0,64},{8,72},{16,80},{24,88},{32,96},{40,104},{48,112},{56,120},{... | collective-permute-start | bytes 884744 | tf_op jit(solution)/shard_map/ppermute | solution.py:25
  474.5 37.5 %collective-permute-start.109 = (bf16[128,1152]{1,0:T(8,128)(2,1)S(1)}, bf16[128,1152]{1,0:T(8,128)(2,1)}, u32[]{:S(2)}, u32[]{:S(2)}) collective-permute-start(bf16[128,1152]{1,0:T(8,128)(2,1)S(1)} %reduce-precision_convert_fusion), channel_id=1, source_target_pairs={{0,96},{8,104},{16,112},{24,120},{32,0},{40,8},{48,16},{56,24},{64... | collective-permute-start | bytes 884744 | tf_op jit(solution)/shard_map/ppermute | solution.py:25
  508.2 37.1 %collective-permute-start.82 = (bf16[1024,128]{1,0:T(8,128)(2,1)}, bf16[1024,128]{1,0:T(8,128)(2,1)}, u32[]{:S(2)}, u32[]{:S(2)}) collective-permute-start(bf16[1024,128]{1,0:T(8,128)(2,1)} %slice_bitcast_fusion.36), channel_id=1, source_target_pairs={{0,8},{8,0},{16,24},{24,16},{32,40},{40,32},{48,56},{56,48},{64,72... | collective-permute-start | bytes 786440 | tf_op jit(solution)/shard_map/ppermute | solution.py:25
  531.1 60.3 %collective-permute-start.66 = (bf16[3,192,1024]{2,1,0:T(8,128)(2,1)}, bf16[3,192,1024]{2,1,0:T(8,128)(2,1)}, u32[]{:S(2)}, u32[]{:S(2)}) collective-permute-start(bf16[3,192,1024]{2,1,0:T(8,128)(2,1)} %slice_bitcast_fusion), channel_id=1, source_target_pairs={{0,8},{8,0},{16,24},{24,16},{32,40},{40,32},{48,56},{56,48},{64,72... | collective-permute-start | bytes 3538952 | tf_op jit(solution)/shard_map/ppermute | solution.py:25
  (178 other events, 1670.3 us)

commit v2 on v1

--- a/solution.py
+++ b/solution.py
@@ -44,8 +44,10 @@
 
 
 def gather_group(u):
-    one, two, three = move_ctx(u, dx=1), move_ctx(u, dx=2), move_ctx(u, dx=3)
-    return [[v, move_ctx(v, dc=1)] for v in (u, one, two, three)]
+    home = move_ctx(u, dc=1)
+    away = jnp.stack([move_ctx(u, dx=1), move_ctx(u, dx=2), move_ctx(u, dx=3)])
+    other = move_ctx(away, dc=1)
+    return [[u, home]] + [[away[r], other[r]] for r in range(3)]
 
 
 def joined(blocks):
@@ -84,8 +86,9 @@
 
 def scatter_fsdp(part, y, zl):
     part = part.reshape((4, 2) + part.shape[1:])
-    give = lax.dynamic_index_in_dim(part, 1 - zl, 1, keepdims=False).astype(BF16)
-    keep = lax.dynamic_index_in_dim(part, zl, 1, keepdims=False)
+    low = zl == 0
+    give = jnp.where(low, part[:, 1], part[:, 0]).astype(BF16)
+    keep = jnp.where(low, part[:, 0], part[:, 1])
     acc = keep.astype(F32) + move_fsdp(give, dz=1).astype(F32)
     total = lax.dynamic_index_in_dim(acc, y, 0, keepdims=False)
     low = acc.astype(BF16)
@@ -315,16 +318,17 @@
     norm_ffn = got[:, part_rows, part_rows:].reshape(width).astype(F32)
     norm_query = got[:, part_rows + 1, :8].reshape(64).astype(F32)
     norm_key = got[:, part_rows + 1, 8:16].reshape(64).astype(F32)
-    out_cols = gather_fsdp(half(w_out, 128), y, zl).reshape(width, 128)
+    gate_up = jnp.concatenate(
+        [half(w_gate, hid), half(w_up, hid), half(w_out, 128)], axis=1
+    )
+    gate_up = gather_fsdp(gate_up, y, zl).reshape(width, 2 * hid + 128)
+    gate_up, out_cols = gate_up[:, : 2 * hid], gate_up[:, 2 * hid :]
     full_out = jnp.zeros((width, width), BF16)
     for r, pair in enumerate(gather_group(out_cols)):
         both = jnp.concatenate(
             [jnp.where(first, pair[0], pair[1]), jnp.where(first, pair[1], pair[0])], axis=1
         )
         full_out = lax.dynamic_update_slice_in_dim(full_out, both, ((x - r) % 4) * 256, 1)
-    gate_up = jnp.concatenate([half(w_gate, hid), half(w_up, hid)], axis=1)
-    gate_up = gather_fsdp(gate_up, y, zl).reshape(width, 2 * hid)
-    w_gate_t, w_up_t = gate_up[:, :hid], gate_up[:, hid:]
     down_rows = hid // 8
     down = swap_roles(lax.dynamic_slice_in_dim(w_down, t * down_rows, down_rows, 0))
     w_down_t = gather_fsdp(down, y, zl).reshape(hid, width)
@@ -390,8 +394,8 @@
     mlp_own = (hidden * scale_ffn * norm_ffn).astype(BF16)
 
     mlp_input = joined(gather_group(mlp_own))
-    gate_proj = plain_dot(mlp_input, w_gate_t)
-    up_proj = plain_dot(mlp_input, w_up_t)
+    both_proj = plain_dot(mlp_input, gate_up)
+    gate_proj, up_proj = both_proj[:, :hid], both_proj[:, hid:]
     grad_mlp = back_dot(grad_output, w_down_t)
     gate_sigmoid = jax.nn.sigmoid(gate_proj)
     mlp_hidden = (gate_proj * gate_sigmoid * up_proj).astype(BF16)
@@ -399,7 +403,8 @@
         grad_mlp * up_proj * gate_sigmoid * (1.0 + gate_proj * (1.0 - gate_sigmoid))
     ).astype(BF16)
     grad_up_low = (grad_mlp * gate_proj * gate_sigmoid).astype(BF16)
-    grad_in_part = back_dot(grad_gate_low, w_gate_t) + back_dot(grad_up_low, w_up_t)
+    grad_both_low = jnp.concatenate([grad_gate_low, grad_up_low], axis=1)
+    grad_in_part = back_dot(grad_both_low, gate_up)
     split = lambda v: v.reshape((4, 2, rows) + v.shape[1:])
     grad_mlp_input = scatter_group(split(grad_in_part.astype(BF16)))
     grad_hidden = cotangent[0].astype(F32) + norm_back(
@@ -452,13 +457,9 @@
     result = (hidden + result).astype(BF16)
 
     grad_down = trans_dot(mlp_hidden, grad_output)
-    grad_gate_w = trans_dot(mlp_input, grad_gate_low)
-    grad_up_w = trans_dot(mlp_input, grad_up_low)
-    sum_ffn_gain = (
-        jnp.sum(grad_gate_w * w_gate_t.astype(F32), axis=1)
-        + jnp.sum(grad_up_w * w_up_t.astype(F32), axis=1)
-    ) / norm_ffn
-    grad_gu = jnp.concatenate([grad_gate_w.astype(BF16), grad_up_w.astype(BF16)], axis=1)
+    grad_gu = trans_dot(mlp_input, grad_both_low)
+    sum_ffn_gain = jnp.sum(grad_gu * gate_up.astype(F32), axis=1) / norm_ffn
+    grad_gu = grad_gu.astype(BF16)
     piece_gu = sum_z(scatter_fsdp(grad_gu.reshape(8, part_rows, 2 * hid), y, zl))
     piece_down = sum_z(scatter_fsdp(grad_down.astype(BF16).reshape(8, down_rows, width), y, zl))
     piece_down = swap_roles(piece_down)
@@ -473,7 +474,7 @@
     grad_out_t = scatter_group(
         jnp.stack([jnp.stack([out_block(r, s) for s in range(2)]) for r in range(4)])
     )
-    piece_out = sum_z(scatter_fsdp(grad_out_t.astype(BF16).reshape(8, part_rows, 128), y, zl))
+    grad_out_t = jnp.pad(grad_out_t.reshape(8, part_rows, 128), ((0, 0), (0, 16), (0, 0)))
 
     grad_qkv_w = trans_dot(normed, qkv_back)
     sum_attn_gain = jnp.sum(grad_qkv_w * w_qkv.astype(F32), axis=1) / norm_attn
@@ -497,7 +498,8 @@
         ],
         axis=1,
     )
-    piece_qkv = sum_z(scatter_fsdp(piece_qkv.astype(BF16), y, zl))
+    piece_qkv = jnp.concatenate([piece_qkv, grad_out_t], axis=2).astype(BF16)
+    piece_qkv = sum_z(scatter_fsdp(piece_qkv, y, zl))
 
     def in_order(piece):
         for r, (own, oth) in enumerate(gather_group(piece)):
@@ -521,15 +523,17 @@
             ((x - r) % 4) * (2 * down_rows),
             0,
         )
-    total_out = columns(in_order(piece_out), 128)
     qkv_pieces = list(in_order(piece_qkv))
     rows_of = slice(0, part_rows)
+    total_out = columns([(r, a[rows_of, 256:], b[rows_of, 256:]) for r, a, b in qkv_pieces], 128)
     total_query = columns([(r, a[rows_of, :128], b[rows_of, :128]) for r, a, b in qkv_pieces], 128)
     total_key = columns([(r, a[rows_of, 128:192], b[rows_of, 128:192]) for r, a, b in qkv_pieces], 64)
-    total_value = columns([(r, a[rows_of, 192:], b[rows_of, 192:]) for r, a, b in qkv_pieces], 64)
+    total_value = columns([(r, a[rows_of, 192:256], b[rows_of, 192:256]) for r, a, b in qkv_pieces], 64)
     extra = jnp.zeros((8, 2, 256), F32)
     for r, a, b in qkv_pieces:
-        both = jnp.stack([a[part_rows : part_rows + 2], b[part_rows : part_rows + 2]]).astype(F32)
+        both = jnp.stack(
+            [a[part_rows : part_rows + 2, :256], b[part_rows : part_rows + 2, :256]]
+        ).astype(F32)
         extra = lax.dynamic_update_slice_in_dim(extra, both, ((x - r) % 4) * 2, 0)
     extra = jnp.sum(extra, axis=0)
     return (

time: 630 us -> 585 us (0.929)
  local copies, waits for them, and re-layouts: 123 us -> 84.7 us
  starting transfers between devices: 172 us -> 148 us
  waiting for transfers between devices: 174 us -> 196 us
    ppermute x32 -> x24, waiting for transfers between devices: 45.5 us -> 68 us  [move_fsdp(): return lax.ppermute(v, 'fsdp', pairs)]
    ppermute x32 -> x24, starting transfers between devices: 46 us -> 34.9 us  [move_fsdp(): return lax.ppermute(v, 'fsdp', pairs)]
    another operation x16 -> x14, local copies, waits for them, and re-layouts: 12.1 us -> 2.23 us  [the longest x1 5.74 us: scatter_fsdp(): part = part.reshape((4, 2) + part.shape[1:])]
    broadcast_in_dim x4 -> x1, local copies, waits for them, and re-layouts: 9.45 us -> 0.01 us  [local(): jnp.zeros((8, 14, 256), F32)]
    dynamic_update_slice x24, other arithmetic: 8.23 us -> 17.5 us  [columns(): lax.dynamic_update_slice_in_dim(full, both, (x - r) % 4 * (2 * size), 1)]
    ppermute x2, starting transfers between devices: 14 us -> 6.34 us  [swap_roles(): return lax.ppermute(v, ('ctx', 'fsdp'), pairs)]
    slice x16 -> x17, local copies, waits for them, and re-layouts: 0.69 us -> 8.18 us  [the longest x4 2.18 us: local(): b[rows_of, 192:256]]
    another operation x4 -> x12, other arithmetic: 0.93 us -> 8.09 us  [the longest x7 5.82 us: gather_group(): away = jnp.stack([move_ctx(u, dx=1), move_ctx(u, dx=2), move_ctx(u, dx=3)])]
  transfers between devices with their start and end apart: 124 -> 94, of which waited for: 43 -> 39; matrix products, arithmetic and copies ran while one was open for 33% -> 27% of each run, Pallas kernels for 5% -> 5%
where the time goes in v2:
time: 585 us; the launch traced here: 574 us
  waiting for transfers between devices  196 us (34%)
  starting transfers between devices  148 us (25%)
  local copies, waits for them, and re-layouts  84.7 us (14%)
  other arithmetic  80.3 us (14%)
  matrix products  33 us (6%)
  Pallas kernels  28.8 us (5%)
    ppermute x68, waiting for transfers between devices, move_ctx(): return lax.ppermute(v, 'ctx', pairs)  125 us
    ppermute x68, starting transfers between devices, move_ctx(): return lax.ppermute(v, 'ctx', pairs)  107 us
    ppermute x24, waiting for transfers between devices, move_fsdp(): return lax.ppermute(v, 'fsdp', pairs)  68 us
    ppermute x24, starting transfers between devices, move_fsdp(): return lax.ppermute(v, 'fsdp', pairs)  34.9 us
    unnamed x200, local copies, waits for them, and re-layouts  28.1 us
    pallas_call x1, Pallas kernels, attend_back(): pl.pallas_call(attend_back_kernel, grid_spec=pltpu.PrefetchScalarGridSpec...  17.5 us
    dynamic_update_slice x24, other arithmetic, columns(): lax.dynamic_update_slice_in_dim(full, both, (x - r) % 4 * (2 * size), 1)  17.5 us
    dot_general x4, matrix products, trans_dot(): lax.dot_general(left, right, (((0,), (0,)), ((), ())), preferred_element_...  12.1 us
  transfers between devices with their start and end apart: 94, of which 39 were waited for; matrix products, arithmetic and copies ran while one was open for 27% of the time, Pallas kernels for 5%

profile of v2, /device:TPU:1, one launch (start us, length us, event | category | flops | bytes accessed | tf_op | source)
XLA Modules:
  0.0 574.4 jit_solution(16009399233511873399)
XLA Ops:
  61.3 5.8 %collective-permute-start.2 = (bf16[208,1024]{1,0:T(8,128)(2,1)S(1)}, bf16[208,1024]{1,0:T(8,128)(2,1)S(1)}, u32[]{:S(2)}, u32[]{:S(2)}) collective-permute-start(bf16[208,1024]{1,0:T(8,128)(2,1)S(1)} %fusion.69), channel_id=1, source_target_pairs={{0,64},{8,72},{16,80},{24,88},{32,96},{40,104},{48,112},{56,120},{... | collective-permute-start | bytes 1277960 | tf_op jit(solution)/shard_map/ppermute | solution.py:25
  73.1 12.8 %collective-permute-done.3 = bf16[208,1024]{1,0:T(8,128)(2,1)S(1)} collective-permute-done((bf16[208,1024]{1,0:T(8,128)(2,1)S(1)}, bf16[208,1024]{1,0:T(8,128)(2,1)S(1)}, u32[]{:S(2)}, u32[]{:S(2)}) %collective-permute-start.3) | collective-permute-done | bytes 426016 | tf_op jit(solution)/shard_map/ppermute | solution.py:25
  91.2 11.3 %collective-permute-done.15 = bf16[2,128,1280]{2,1,0:T(8,128)(2,1)S(1)} collective-permute-done((bf16[2,128,1280]{2,1,0:T(8,128)(2,1)S(1)}, bf16[2,128,1280]{2,1,0:T(8,128)(2,1)S(1)}, u32[]{:S(2)}, u32[]{:S(2)}) %collective-permute-start.15) | collective-permute-done | bytes 655392 | tf_op jit(solution)/shard_map/ppermute | solution.py:32
  104.9 12.3 %collective-permute-done.16 = bf16[2,128,1280]{2,1,0:T(8,128)(2,1)S(1)} collective-permute-done((bf16[2,128,1280]{2,1,0:T(8,128)(2,1)S(1)}, bf16[2,128,1280]{2,1,0:T(8,128)(2,1)S(1)}, u32[]{:S(2)}, u32[]{:S(2)}) %collective-permute-start.16) | collective-permute-done | bytes 655392 | tf_op jit(solution)/shard_map/ppermute | solution.py:32
  125.6 4.6 collective-permute-start.32
  177.9 11.2 %attend.1 = (f32[4,384,128]{2,1,0:T(8,128)}, bf16[4,384,128]{2,1,0:T(8,128)(2,1)}, f32[4,1,768]{2,1,0:T(1,128)}) custom-call(s32[6]{0:T(128)} %pad_add_fusion.5.meta, bf16[2,4,384,64]{3,2,1,0:T(8,128)(2,1)} %bitcast.727, bf16[8,384,64]{2,1,0:T(8,128)(2,1)} %get-tuple-element.127.k_ref, bf16[8,384,128]{2,1,0:T(8,128)(2,1)} %maximum_maximum_fusion.v_ref, ...), custom_call_target="tpu_custom_call" | custom-call | flops 4000000000 | bytes 6000000 | tf_op jit(solution)/shard_map/attend/pallas_call | solution.py:172
  214.1 10.1 %collective-permute-done.25 = bf16[192,1024]{1,0:T(8,128)(2,1)S(1)} collective-permute-done((bf16[192,1024]{1,0:T(8,128)(2,1)}, bf16[192,1024]{1,0:T(8,128)(2,1)S(1)}, u32[]{:S(2)}, u32[]{:S(2)}) %collective-permute-start.25) | collective-permute-done | bytes 393248 | tf_op jit(solution)/shard_map/ppermute | solution.py:25
  245.3 6.2 %fusion.5 = f32[1536,1152]{0,1:T(8,128)S(1)} fusion(bf16[1536,1024]{1,0:T(8,128)(2,1)} %fusion.75, bf16[1024,1280]{1,0:T(8,128)(2,1)S(1)} %bitcast.696), kind=kOutput, calls=%fused_computation.22 | convolution fusion | flops 3623878656 | bytes 12582912 | tf_op jit(solution)/shard_map/dot_general | solution.py:124
  255.1 5.3 fusion.112
  271.8 9.8 %collective-permute-done.83 = bf16[4,72,1024]{2,1,0:T(8,128)(2,1)S(1)} collective-permute-done((bf16[4,72,1024]{2,1,0:T(8,128)(2,1)S(1)}, bf16[4,72,1024]{2,1,0:T(8,128)(2,1)S(1)}, u32[]{:S(2)}, u32[]{:S(2)}) %collective-permute-start.83) | collective-permute-done | bytes 589856 | tf_op jit(solution)/shard_map/ppermute | solution.py:32
  292.5 4.7 collective-permute-start.87
  297.3 17.7 %collective-permute-done.87 = bf16[72,1024]{1,0:T(8,128)(2,1)S(1)} collective-permute-done((bf16[72,1024]{1,0:T(8,128)(2,1)S(1)}, bf16[72,1024]{1,0:T(8,128)(2,1)S(1)}, u32[]{:S(2)}, u32[]{:S(2)}) %collective-permute-start.87) | collective-permute-done | bytes 147488 | tf_op jit(solution)/shard_map/ppermute | solution.py:25
  324.4 9.0 %collective-permute-start.91 = (bf16[72,1024]{1,0:T(8,128)(2,1)S(1)}, bf16[72,1024]{1,0:T(8,128)(2,1)S(1)}, u32[]{:S(2)}, u32[]{:S(2)}) collective-permute-start(bf16[72,1024]{1,0:T(8,128)(2,1)S(1)} %collective-permute-done.88), channel_id=1, source_target_pairs={{0,64},{8,72},{16,80},{24,88},{32,96},{40,104},{48,112},{56,120},{... | collective-permute-start | bytes 442376 | tf_op jit(solution)/shard_map/ppermute | solution.py:25
  346.7 11.9 %collective-permute-done.74 = bf16[128,1152]{1,0:T(8,128)(2,1)S(1)} collective-permute-done((bf16[128,1152]{1,0:T(8,128)(2,1)S(1)}, bf16[128,1152]{1,0:T(8,128)(2,1)S(1)}, u32[]{:S(2)}, u32[]{:S(2)}) %collective-permute-start.74) | collective-permute-done | bytes 294944 | tf_op jit(solution)/shard_map/ppermute | solution.py:32
  362.2 6.3 %collective-permute-done.45 = bf16[192,1024]{1,0:T(8,128)(2,1)S(1)} collective-permute-done((bf16[192,1024]{1,0:T(8,128)(2,1)S(1)}, bf16[192,1024]{1,0:T(8,128)(2,1)S(1)}, u32[]{:S(2)}, u32[]{:S(2)}) %collective-permute-start.45) | collective-permute-done | bytes 393248 | tf_op jit(solution)/shard_map/ppermute | solution.py:25
  369.5 12.9 %collective-permute-done.47 = bf16[192,1024]{1,0:T(8,128)(2,1)S(1)} collective-permute-done((bf16[192,1024]{1,0:T(8,128)(2,1)S(1)}, bf16[192,1024]{1,0:T(8,128)(2,1)S(1)}, u32[]{:S(2)}, u32[]{:S(2)}) %collective-permute-start.47) | collective-permute-done | bytes 393248 | tf_op jit(solution)/shard_map/ppermute | solution.py:25
  385.4 11.2 %collective-permute-done.37 = bf16[192,1024]{1,0:T(8,128)(2,1)S(1)} collective-permute-done((bf16[192,1024]{1,0:T(8,128)(2,1)S(1)}, bf16[192,1024]{1,0:T(8,128)(2,1)S(1)}, u32[]{:S(2)}, u32[]{:S(2)}) %collective-permute-start.37) | collective-permute-done | bytes 393248 | tf_op jit(solution)/shard_map/ppermute | solution.py:25
  406.4 11.4 %collective-permute-done.49 = bf16[2,192,128]{2,1,0:T(8,128)(2,1)S(1)} collective-permute-done((bf16[2,192,128]{2,1,0:T(8,128)(2,1)S(1)}, bf16[2,192,128]{2,1,0:T(8,128)(2,1)S(1)}, u32[]{:S(2)}, u32[]{:S(2)}) %collective-permute-start.49) | collective-permute-done | bytes 98336 | tf_op jit(solution)/shard_map/ppermute | solution.py:25
  417.9 4.9 collective-permute-done.50
  427.8 17.5 %attend_back.1 = (f32[2,4,384,64]{3,2,1,0:T(8,128)}, f32[8,384,64]{2,1,0:T(8,128)}, f32[8,384,64]{2,1,0:T(8,128)}) custom-call(s32[6]{0:T(128)} %pad_add_fusion.5.meta, bf16[2,4,384,64]{3,2,1,0:T(8,128)(2,1)} %bitcast.728, bf16[4,384,128]{2,1,0:T(8,128)(2,1)} %bitcast.736, bf16[8,384,64]{2,1,0:T(8,128)(2,1)} %get-tuple-element.127.k_ref, ...), custom_call_target="tpu_custom_call" | custom-call | flops 10000000000 | bytes 9000000 | tf_op jit(solution)/shard_map/attend_back/pallas_call | solution.py:246
  489.7 5.7 collective-permute-start.53
  507.6 5.2 collective-permute-done.63
  520.2 5.1 collective-permute-start.67
  534.1 5.3 collective-permute-done.69
  (683 shorter events, 352.5 us)
Async XLA Ops:
  0.7 60.7 %collective-permute-start.39 = (bf16[192,1024]{1,0:T(8,128)(2,1)}, bf16[192,1024]{1,0:T(8,128)(2,1)S(1)}, u32[]{:S(2)}, u32[]{:S(2)}) collective-permute-start(bf16[192,1024]{1,0:T(8,128)(2,1)} %bitcast.709), channel_id=1, source_target_pairs={{0,32},{8,40},{16,48},{24,56},{32,64},{40,72},{48,80},{56,88},{64,... | collective-permute-start | bytes 1179656 | tf_op jit(solution)/shard_map/ppermute | solution.py:25
  2.8 64.4 %collective-permute-start.40 = (bf16[192,1024]{1,0:T(8,128)(2,1)}, bf16[192,1024]{1,0:T(8,128)(2,1)S(1)}, u32[]{:S(2)}, u32[]{:S(2)}) collective-permute-start(bf16[192,1024]{1,0:T(8,128)(2,1)} %bitcast.710), channel_id=1, source_target_pairs={{0,64},{8,72},{16,80},{24,88},{32,96},{40,104},{48,112},{56,120},{... | collective-permute-start | bytes 1179656 | tf_op jit(solution)/shard_map/ppermute | solution.py:25
  5.2 62.0 %collective-permute-start.41 = (bf16[192,1024]{1,0:T(8,128)(2,1)}, bf16[192,1024]{1,0:T(8,128)(2,1)S(1)}, u32[]{:S(2)}, u32[]{:S(2)}) collective-permute-start(bf16[192,1024]{1,0:T(8,128)(2,1)} %bitcast.711), channel_id=1, source_target_pairs={{0,96},{8,104},{16,112},{24,120},{32,0},{40,8},{48,16},{56,24},{64... | collective-permute-start | bytes 1179656 | tf_op jit(solution)/shard_map/ppermute | solution.py:25
  57.4 29.1 %collective-permute-start.1 = (bf16[208,1024]{1,0:T(8,128)(2,1)S(1)}, bf16[208,1024]{1,0:T(8,128)(2,1)S(1)}, u32[]{:S(2)}, u32[]{:S(2)}) collective-permute-start(bf16[208,1024]{1,0:T(8,128)(2,1)S(1)} %fusion.69), channel_id=1, source_target_pairs={{0,32},{8,40},{16,48},{24,56},{32,64},{40,72},{48,80},{56,88},{64,... | collective-permute-start | bytes 1277960 | tf_op jit(solution)/shard_map/ppermute | solution.py:25
  61.3 29.1 %collective-permute-start.2 = (bf16[208,1024]{1,0:T(8,128)(2,1)S(1)}, bf16[208,1024]{1,0:T(8,128)(2,1)S(1)}, u32[]{:S(2)}, u32[]{:S(2)}) collective-permute-start(bf16[208,1024]{1,0:T(8,128)(2,1)S(1)} %fusion.69), channel_id=1, source_target_pairs={{0,64},{8,72},{16,80},{24,88},{32,96},{40,104},{48,112},{56,120},{... | collective-permute-start | bytes 1277960 | tf_op jit(solution)/shard_map/ppermute | solution.py:25
  67.2 54.8 %collective-permute-start.30 = (bf16[2,72,1024]{2,1,0:T(8,128)(2,1)}, bf16[2,72,1024]{2,1,0:T(8,128)(2,1)S(1)}, u32[]{:S(2)}, u32[]{:S(2)}) collective-permute-start(bf16[2,72,1024]{2,1,0:T(8,128)(2,1)} %pad_maximum_fusion.22), channel_id=1, source_target_pairs={{0,2},{1,3},{2,4},{3,5},{4,6},{5,7},{6,0},{7,1},{8,10},{9,11},{10,... | collective-permute-start | bytes 884744 | tf_op jit(solution)/shard_map/ppermute | solution.py:32
  69.2 53.3 %collective-permute-start.31 = (bf16[2,72,1024]{2,1,0:T(8,128)(2,1)}, bf16[2,72,1024]{2,1,0:T(8,128)(2,1)S(1)}, u32[]{:S(2)}, u32[]{:S(2)}) collective-permute-start(bf16[2,72,1024]{2,1,0:T(8,128)(2,1)} %pad_maximum_fusion.22), channel_id=1, source_target_pairs={{0,4},{1,5},{2,6},{3,7},{4,0},{5,1},{6,2},{7,3},{8,12},{9,13},{10,... | collective-permute-start | bytes 884744 | tf_op jit(solution)/shard_map/ppermute | solution.py:32
  86.5 30.7 %collective-permute-start.16 = (bf16[2,128,1280]{2,1,0:T(8,128)(2,1)S(1)}, bf16[2,128,1280]{2,1,0:T(8,128)(2,1)S(1)}, u32[]{:S(2)}, u32[]{:S(2)}) collective-permute-start(bf16[2,128,1280]{2,1,0:T(8,128)(2,1)S(1)} %pad_maximum_fusion.16), channel_id=1, source_target_pairs={{0,4},{1,5},{2,6},{3,7},{4,0},{5,1},{6,2},{7,3},{8,12},{9,13},{10,... | collective-permute-start | bytes 1966088 | tf_op jit(solution)/shard_map/ppermute | solution.py:32
  102.6 33.8 %collective-permute-start.4 = (bf16[3,208,1024]{2,1,0:T(8,128)(2,1)S(1)}, bf16[3,208,1024]{2,1,0:T(8,128)(2,1)S(1)}, u32[]{:S(2)}, u32[]{:S(2)}) collective-permute-start(bf16[3,208,1024]{2,1,0:T(8,128)(2,1)S(1)} %pad_maximum_fusion.4), channel_id=1, source_target_pairs={{0,8},{8,0},{16,24},{24,16},{32,40},{40,32},{48,56},{56,48},{64,72... | collective-permute-start | bytes 3833864 | tf_op jit(solution)/shard_map/ppermute | solution.py:25
  125.6 81.5 %collective-permute-start.32 = (bf16[2,72,1024]{2,1,0:T(8,128)(2,1)}, bf16[2,72,1024]{2,1,0:T(8,128)(2,1)}, u32[]{:S(2)}, u32[]{:S(2)}) collective-permute-start(bf16[2,72,1024]{2,1,0:T(8,128)(2,1)} %pad_maximum_fusion.22), channel_id=1, source_target_pairs={{0,6},{1,7},{2,0},{3,1},{4,2},{5,3},{6,4},{7,5},{8,14},{9,15},{10,... | collective-permute-start | bytes 884744 | tf_op jit(solution)/shard_map/ppermute | solution.py:32
  132.4 76.4 %collective-permute-start.42 = (bf16[3,192,1024]{2,1,0:T(8,128)(2,1)}, bf16[3,192,1024]{2,1,0:T(8,128)(2,1)}, u32[]{:S(2)}, u32[]{:S(2)}) collective-permute-start(bf16[3,192,1024]{2,1,0:T(8,128)(2,1)} %pad_maximum_fusion.7), channel_id=1, source_target_pairs={{0,8},{8,0},{16,24},{24,16},{32,40},{40,32},{48,56},{56,48},{64,72... | collective-permute-start | bytes 3538952 | tf_op jit(solution)/shard_map/ppermute | solution.py:25
  135.9 30.6 %collective-permute-start.22 = (bf16[3,1024,128]{2,1,0:T(8,128)(2,1)}, bf16[3,1024,128]{2,1,0:T(8,128)(2,1)}, u32[]{:S(2)}, u32[]{:S(2)}) collective-permute-start(bf16[3,1024,128]{2,1,0:T(8,128)(2,1)} %pad_maximum_fusion.14), channel_id=1, source_target_pairs={{0,8},{8,0},{16,24},{24,16},{32,40},{40,32},{48,56},{56,48},{64,72... | collective-permute-start | bytes 2359304 | tf_op jit(solution)/shard_map/ppermute | solution.py:25
  268.2 73.6 %collective-permute-start.73 = (bf16[4,128,1152]{2,1,0:T(8,128)(2,1)S(1)}, bf16[4,128,1152]{2,1,0:T(8,128)(2,1)S(1)}, u32[]{:S(2)}, u32[]{:S(2)}) collective-permute-start(bf16[4,128,1152]{2,1,0:T(8,128)(2,1)S(1)} %fusion.9), channel_id=1, source_target_pairs={{0,1},{1,0},{2,3},{3,2},{4,5},{5,4},{6,7},{7,6},{8,9},{9,8},{10,11... | collective-permute-start | bytes 3538952 | tf_op jit(solution)/shard_map/ppermute | solution.py:32
  287.4 56.6 %collective-permute-start.34 = (bf16[3,192,1024]{2,1,0:T(8,128)(2,1)S(1)}, bf16[3,192,1024]{2,1,0:T(8,128)(2,1)S(1)}, u32[]{:S(2)}, u32[]{:S(2)}) collective-permute-start(bf16[3,192,1024]{2,1,0:T(8,128)(2,1)S(1)} %slice_bitcast_fusion.2), channel_id=1, source_target_pairs={{0,8},{8,0},{16,24},{24,16},{32,40},{40,32},{48,56},{56,48},{64,72... | collective-permute-start | bytes 3538952 | tf_op jit(solution)/shard_map/ppermute | solution.py:25
  336.5 46.3 %collective-permute-start.33 = (bf16[192,1024]{1,0:T(8,128)(2,1)S(1)}, bf16[192,1024]{1,0:T(8,128)(2,1)S(1)}, u32[]{:S(2)}, u32[]{:S(2)}) collective-permute-start(bf16[192,1024]{1,0:T(8,128)(2,1)S(1)} %slice_bitcast_fusion.31), channel_id=1, source_target_pairs={{0,8},{8,0},{16,24},{24,16},{32,40},{40,32},{48,56},{56,48},{64,72... | collective-permute-start | bytes 1179656 | tf_op jit(solution)/shard_map/ppermute | solution.py:25
  360.3 44.6 %collective-permute-start.93 = (bf16[3,72,1024]{2,1,0:T(8,128)(2,1)S(1)}, bf16[3,72,1024]{2,1,0:T(8,128)(2,1)S(1)}, u32[]{:S(2)}, u32[]{:S(2)}) collective-permute-start(bf16[3,72,1024]{2,1,0:T(8,128)(2,1)S(1)} %pad_maximum_fusion.17), channel_id=1, source_target_pairs={{0,8},{8,0},{16,24},{24,16},{32,40},{40,32},{48,56},{56,48},{64,72... | collective-permute-start | bytes 1327112 | tf_op jit(solution)/shard_map/ppermute | solution.py:25
  403.0 81.4 %collective-permute-start.58 = (bf16[1024,128]{1,0:T(8,128)(2,1)}, bf16[1024,128]{1,0:T(8,128)(2,1)}, u32[]{:S(2)}, u32[]{:S(2)}) collective-permute-start(bf16[1024,128]{1,0:T(8,128)(2,1)} %slice_bitcast_fusion.51), channel_id=1, source_target_pairs={{0,8},{8,0},{16,24},{24,16},{32,40},{40,32},{48,56},{56,48},{64,72... | collective-permute-start | bytes 786440 | tf_op jit(solution)/shard_map/ppermute | solution.py:25
  404.4 74.0 %collective-permute-start.59 = (bf16[3,1024,128]{2,1,0:T(8,128)(2,1)}, bf16[3,1024,128]{2,1,0:T(8,128)(2,1)}, u32[]{:S(2)}, u32[]{:S(2)}) collective-permute-start(bf16[3,1024,128]{2,1,0:T(8,128)(2,1)} %fusion.28), channel_id=1, source_target_pairs={{0,8},{8,0},{16,24},{24,16},{32,40},{40,32},{48,56},{56,48},{64,72... | collective-permute-start | bytes 2359304 | tf_op jit(solution)/shard_map/ppermute | solution.py:25
  406.2 42.7 %collective-permute-start.78 = (bf16[128,1152]{1,0:T(8,128)(2,1)}, bf16[128,1152]{1,0:T(8,128)(2,1)}, u32[]{:S(2)}, u32[]{:S(2)}) collective-permute-start(bf16[128,1152]{1,0:T(8,128)(2,1)} %reduce-precision_convert_fusion), channel_id=1, source_target_pairs={{0,8},{8,0},{16,24},{24,16},{32,40},{40,32},{48,56},{56,48},{64,72... | collective-permute-start | bytes 884744 | tf_op jit(solution)/shard_map/ppermute | solution.py:25
  406.2 46.2 %collective-permute-start.79 = (bf16[128,1152]{1,0:T(8,128)(2,1)}, bf16[128,1152]{1,0:T(8,128)(2,1)}, u32[]{:S(2)}, u32[]{:S(2)}) collective-permute-start(bf16[128,1152]{1,0:T(8,128)(2,1)} %reduce-precision_convert_fusion), channel_id=1, source_target_pairs={{0,32},{8,40},{16,48},{24,56},{32,64},{40,72},{48,80},{56,88},{64,... | collective-permute-start | bytes 884744 | tf_op jit(solution)/shard_map/ppermute | solution.py:25
  426.3 30.3 %collective-permute-start.80 = (bf16[128,1152]{1,0:T(8,128)(2,1)}, bf16[128,1152]{1,0:T(8,128)(2,1)}, u32[]{:S(2)}, u32[]{:S(2)}) collective-permute-start(bf16[128,1152]{1,0:T(8,128)(2,1)} %reduce-precision_convert_fusion), channel_id=1, source_target_pairs={{0,64},{8,72},{16,80},{24,88},{32,96},{40,104},{48,112},{56,120},{... | collective-permute-start | bytes 884744 | tf_op jit(solution)/shard_map/ppermute | solution.py:25
  458.8 43.4 %collective-permute-start.82 = (bf16[3,128,1152]{2,1,0:T(8,128)(2,1)}, bf16[3,128,1152]{2,1,0:T(8,128)(2,1)}, u32[]{:S(2)}, u32[]{:S(2)}) collective-permute-start(bf16[3,128,1152]{2,1,0:T(8,128)(2,1)} %pad_maximum_fusion.9), channel_id=1, source_target_pairs={{0,8},{8,0},{16,24},{24,16},{32,40},{40,32},{48,56},{56,48},{64,72... | collective-permute-start | bytes 2654216 | tf_op jit(solution)/shard_map/ppermute | solution.py:25
  484.4 57.9 %collective-permute-start.54 = (bf16[3,192,1024]{2,1,0:T(8,128)(2,1)S(1)}, bf16[3,192,1024]{2,1,0:T(8,128)(2,1)S(1)}, u32[]{:S(2)}, u32[]{:S(2)}) collective-permute-start(bf16[3,192,1024]{2,1,0:T(8,128)(2,1)S(1)} %slice_bitcast_fusion), channel_id=1, source_target_pairs={{0,8},{8,0},{16,24},{24,16},{32,40},{40,32},{48,56},{56,48},{64,72... | collective-permute-start | bytes 3538952 | tf_op jit(solution)/shard_map/ppermute | solution.py:25
  489.7 80.5 %collective-permute-start.53 = (bf16[192,1024]{1,0:T(8,128)(2,1)}, bf16[192,1024]{1,0:T(8,128)(2,1)S(1)}, u32[]{:S(2)}, u32[]{:S(2)}) collective-permute-start(bf16[192,1024]{1,0:T(8,128)(2,1)} %slice_bitcast_fusion.12), channel_id=1, source_target_pairs={{0,8},{8,0},{16,24},{24,16},{32,40},{40,32},{48,56},{56,48},{64,72... | collective-permute-start | bytes 1179656 | tf_op jit(solution)/shard_map/ppermute | solution.py:25
  (156 other events, 1594.8 us)

commit v3 on v2

--- a/solution.py
+++ b/solution.py
@@ -55,11 +55,10 @@
 
 
 def scatter_group(part):
-    other = move_ctx(part[1:, 1].astype(BF16), dc=1)
-    other_home = move_ctx(part[0, 1].astype(BF16), dc=1)
-    total = part[0, 0].astype(F32) + other_home.astype(F32)
+    other = move_ctx(part[:, 1].astype(BF16), dc=1)
+    total = part[0, 0].astype(F32) + other[0].astype(F32)
     for r in (1, 2, 3):
-        acc = part[r, 0].astype(F32) + other[r - 1].astype(F32)
+        acc = part[r, 0].astype(F32) + other[r].astype(F32)
         total = total + move_ctx(acc.astype(BF16), dx=-r).astype(F32)
     return total
 

time: 585 us -> 564 us (0.964)
  waiting for transfers between devices: 196 us -> 171 us
  starting transfers between devices: 148 us -> 162 us
  other arithmetic: 80.3 us -> 74.1 us
    ppermute x68 -> x64, waiting for transfers between devices: 125 us -> 103 us  [move_ctx(): return lax.ppermute(v, 'ctx', pairs)]
    ppermute x68 -> x64, starting transfers between devices: 107 us -> 120 us  [move_ctx(): return lax.ppermute(v, 'ctx', pairs)]
    unnamed x200 -> x212, local copies, waits for them, and re-layouts: 28.1 us -> 32.3 us
  transfers between devices with their start and end apart: 94 -> 90, of which waited for: 39 -> 36; matrix products, arithmetic and copies ran while one was open for 27% -> 28% of each run, Pallas kernels for 5% -> 5%
where the time goes in v3:
time: 564 us; the launch traced here: 555 us
  waiting for transfers between devices  171 us (30%)
  starting transfers between devices  162 us (29%)
  local copies, waits for them, and re-layouts  82 us (15%)
  other arithmetic  74.1 us (13%)
  matrix products  33 us (6%)
  Pallas kernels  28.8 us (5%)
    ppermute x64, starting transfers between devices, move_ctx(): return lax.ppermute(v, 'ctx', pairs)  120 us
    ppermute x64, waiting for transfers between devices, move_ctx(): return lax.ppermute(v, 'ctx', pairs)  103 us
    ppermute x24, waiting for transfers between devices, move_fsdp(): return lax.ppermute(v, 'fsdp', pairs)  65.5 us
    ppermute x24, starting transfers between devices, move_fsdp(): return lax.ppermute(v, 'fsdp', pairs)  34.6 us
    unnamed x212, local copies, waits for them, and re-layouts  32.3 us
    pallas_call x1, Pallas kernels, attend_back(): pl.pallas_call(attend_back_kernel, grid_spec=pltpu.PrefetchScalarGridSpec...  17.5 us
    dynamic_update_slice x24, other arithmetic, columns(): lax.dynamic_update_slice_in_dim(full, both, (x - r) % 4 * (2 * size), 1)  14 us
    dot_general x4, matrix products, trans_dot(): lax.dot_general(left, right, (((0,), (0,)), ((), ())), preferred_element_...  12.1 us
  transfers between devices with their start and end apart: 90, of which 36 were waited for; matrix products, arithmetic and copies ran while one was open for 28% of the time, Pallas kernels for 5%

profile of v3, /device:TPU:1, one launch (start us, length us, event | category | flops | bytes accessed | tf_op | source)
XLA Modules:
  0.0 554.7 jit_solution(1558157216659003025)
XLA Ops:
  61.3 5.8 %collective-permute-start.2 = (bf16[208,1024]{1,0:T(8,128)(2,1)S(1)}, bf16[208,1024]{1,0:T(8,128)(2,1)S(1)}, u32[]{:S(2)}, u32[]{:S(2)}) collective-permute-start(bf16[208,1024]{1,0:T(8,128)(2,1)S(1)} %fusion.69), channel_id=1, source_target_pairs={{0,64},{8,72},{16,80},{24,88},{32,96},{40,104},{48,112},{56,120},{... | collective-permute-start | bytes 1277960 | tf_op jit(solution)/shard_map/ppermute | solution.py:25
  73.0 12.8 %collective-permute-done.3 = bf16[208,1024]{1,0:T(8,128)(2,1)S(1)} collective-permute-done((bf16[208,1024]{1,0:T(8,128)(2,1)S(1)}, bf16[208,1024]{1,0:T(8,128)(2,1)S(1)}, u32[]{:S(2)}, u32[]{:S(2)}) %collective-permute-start.3) | collective-permute-done | bytes 426016 | tf_op jit(solution)/shard_map/ppermute | solution.py:25
  91.1 11.4 %collective-permute-done.15 = bf16[2,128,1280]{2,1,0:T(8,128)(2,1)S(1)} collective-permute-done((bf16[2,128,1280]{2,1,0:T(8,128)(2,1)S(1)}, bf16[2,128,1280]{2,1,0:T(8,128)(2,1)S(1)}, u32[]{:S(2)}, u32[]{:S(2)}) %collective-permute-start.15) | collective-permute-done | bytes 655392 | tf_op jit(solution)/shard_map/ppermute | solution.py:32
  104.9 12.3 %collective-permute-done.16 = bf16[2,128,1280]{2,1,0:T(8,128)(2,1)S(1)} collective-permute-done((bf16[2,128,1280]{2,1,0:T(8,128)(2,1)S(1)}, bf16[2,128,1280]{2,1,0:T(8,128)(2,1)S(1)}, u32[]{:S(2)}, u32[]{:S(2)}) %collective-permute-start.16) | collective-permute-done | bytes 655392 | tf_op jit(solution)/shard_map/ppermute | solution.py:32
  125.5 4.6 collective-permute-start.32
  177.7 11.2 %attend.1 = (f32[4,384,128]{2,1,0:T(8,128)}, bf16[4,384,128]{2,1,0:T(8,128)(2,1)}, f32[4,1,768]{2,1,0:T(1,128)}) custom-call(s32[6]{0:T(128)} %pad_add_fusion.5.meta, bf16[2,4,384,64]{3,2,1,0:T(8,128)(2,1)} %bitcast.746, bf16[8,384,64]{2,1,0:T(8,128)(2,1)} %get-tuple-element.127.k_ref, bf16[8,384,128]{2,1,0:T(8,128)(2,1)} %maximum_maximum_fusion.v_ref, ...), custom_call_target="tpu_custom_call" | custom-call | flops 4000000000 | bytes 6000000 | tf_op jit(solution)/shard_map/attend/pallas_call | solution.py:171
  213.8 10.2 %collective-permute-done.25 = bf16[192,1024]{1,0:T(8,128)(2,1)S(1)} collective-permute-done((bf16[192,1024]{1,0:T(8,128)(2,1)}, bf16[192,1024]{1,0:T(8,128)(2,1)S(1)}, u32[]{:S(2)}, u32[]{:S(2)}) %collective-permute-start.25) | collective-permute-done | bytes 393248 | tf_op jit(solution)/shard_map/ppermute | solution.py:25
  245.0 6.2 %fusion.5 = f32[1536,1152]{0,1:T(8,128)S(1)} fusion(bf16[1536,1024]{1,0:T(8,128)(2,1)} %fusion.75, bf16[1024,1280]{1,0:T(8,128)(2,1)S(1)} %bitcast.714), kind=kOutput, calls=%fused_computation.22 | convolution fusion | flops 3623878656 | bytes 12582912 | tf_op jit(solution)/shard_map/dot_general | solution.py:123
  258.4 5.3 fusion.112
  264.3 4.5 convolution_convert_fusion.2
  281.0 5.3 collective-permute-start.83
  289.7 14.2 %collective-permute-done.83 = bf16[72,1024]{1,0:T(8,128)(2,1)S(1)} collective-permute-done((bf16[72,1024]{1,0:T(8,128)(2,1)S(1)}, bf16[72,1024]{1,0:T(8,128)(2,1)S(1)}, u32[]{:S(2)}, u32[]{:S(2)}) %collective-permute-start.83) | collective-permute-done | bytes 147488 | tf_op jit(solution)/shard_map/ppermute | solution.py:25
  312.1 9.1 %collective-permute-start.87 = (bf16[72,1024]{1,0:T(8,128)(2,1)S(1)}, bf16[72,1024]{1,0:T(8,128)(2,1)S(1)}, u32[]{:S(2)}, u32[]{:S(2)}) collective-permute-start(bf16[72,1024]{1,0:T(8,128)(2,1)S(1)} %collective-permute-done.84), channel_id=1, source_target_pairs={{0,64},{8,72},{16,80},{24,88},{32,96},{40,104},{48,112},{56,120},{... | collective-permute-start | bytes 442376 | tf_op jit(solution)/shard_map/ppermute | solution.py:25
  338.2 6.7 %collective-permute-done.71 = bf16[128,1152]{1,0:T(8,128)(2,1)S(1)} collective-permute-done((bf16[128,1152]{1,0:T(8,128)(2,1)S(1)}, bf16[128,1152]{1,0:T(8,128)(2,1)S(1)}, u32[]{:S(2)}, u32[]{:S(2)}) %collective-permute-start.71) | collective-permute-done | bytes 294944 | tf_op jit(solution)/shard_map/ppermute | solution.py:32
  354.7 17.8 %collective-permute-done.43 = bf16[192,1024]{1,0:T(8,128)(2,1)S(1)} collective-permute-done((bf16[192,1024]{1,0:T(8,128)(2,1)S(1)}, bf16[192,1024]{1,0:T(8,128)(2,1)S(1)}, u32[]{:S(2)}, u32[]{:S(2)}) %collective-permute-start.43) | collective-permute-done | bytes 393248 | tf_op jit(solution)/shard_map/ppermute | solution.py:25
  375.5 6.4 %collective-permute-start.75 = (bf16[128,1152]{1,0:T(8,128)(2,1)S(1)}, bf16[128,1152]{1,0:T(8,128)(2,1)S(1)}, u32[]{:S(2)}, u32[]{:S(2)}) collective-permute-start(bf16[128,1152]{1,0:T(8,128)(2,1)S(1)} %reduce-precision_convert_fusion), channel_id=1, source_target_pairs={{0,32},{8,40},{16,48},{24,56},{32,64},{40,72},{48,80},{56,88},{64,... | collective-permute-start | bytes 884744 | tf_op jit(solution)/shard_map/ppermute | solution.py:25
  393.9 5.7 %collective-permute-done.76 = bf16[128,1152]{1,0:T(8,128)(2,1)S(1)} collective-permute-done((bf16[128,1152]{1,0:T(8,128)(2,1)S(1)}, bf16[128,1152]{1,0:T(8,128)(2,1)S(1)}, u32[]{:S(2)}, u32[]{:S(2)}) %collective-permute-start.76) | collective-permute-done | bytes 294944 | tf_op jit(solution)/shard_map/ppermute | solution.py:25
  404.9 7.3 %collective-permute-done.47 = bf16[2,192,128]{2,1,0:T(8,128)(2,1)S(1)} collective-permute-done((bf16[2,192,128]{2,1,0:T(8,128)(2,1)S(1)}, bf16[2,192,128]{2,1,0:T(8,128)(2,1)S(1)}, u32[]{:S(2)}, u32[]{:S(2)}) %collective-permute-start.47) | collective-permute-done | bytes 98336 | tf_op jit(solution)/shard_map/ppermute | solution.py:25
  413.7 17.5 %attend_back.1 = (f32[2,4,384,64]{3,2,1,0:T(8,128)}, f32[8,384,64]{2,1,0:T(8,128)}, f32[8,384,64]{2,1,0:T(8,128)}) custom-call(s32[6]{0:T(128)} %pad_add_fusion.5.meta, bf16[2,4,384,64]{3,2,1,0:T(8,128)(2,1)} %bitcast.747, bf16[4,384,128]{2,1,0:T(8,128)(2,1)} %bitcast.755, bf16[8,384,64]{2,1,0:T(8,128)(2,1)} %get-tuple-element.127.k_ref, ...), custom_call_target="tpu_custom_call" | custom-call | flops 10000000000 | bytes 9000000 | tf_op jit(solution)/shard_map/attend_back/pallas_call | solution.py:245
  434.1 7.3 %collective-permute-start.50 = (bf16[4,384,128]{2,1,0:T(8,128)(2,1)}, bf16[4,384,128]{2,1,0:T(8,128)(2,1)}, u32[]{:S(2)}, u32[]{:S(2)}) collective-permute-start(bf16[4,384,128]{2,1,0:T(8,128)(2,1)} %fusion.29), channel_id=1, source_target_pairs={{0,16},{8,24},{16,0},{24,8},{32,48},{40,56},{48,32},{56,40},{64,80... | collective-permute-start | bytes 1179656 | tf_op jit(solution)/shard_map/ppermute | solution.py:25
  471.2 4.9 collective-permute-done.56
  477.5 7.4 %collective-permute-done.58 = bf16[1024,128]{1,0:T(8,128)(2,1)S(1)} collective-permute-done((bf16[1024,128]{1,0:T(8,128)(2,1)S(1)}, bf16[1024,128]{1,0:T(8,128)(2,1)S(1)}, u32[]{:S(2)}, u32[]{:S(2)}) %collective-permute-start.58) | collective-permute-done | bytes 262176 | tf_op jit(solution)/shard_map/ppermute | solution.py:25
  486.8 11.0 %collective-permute-done.59 = bf16[4,144,384]{2,1,0:T(8,128)(2,1)S(1)} collective-permute-done((bf16[4,144,384]{2,1,0:T(8,128)(2,1)S(1)}, bf16[4,144,384]{2,1,0:T(8,128)(2,1)S(1)}, u32[]{:S(2)}, u32[]{:S(2)}) %collective-permute-start.59) | collective-permute-done | bytes 442400 | tf_op jit(solution)/shard_map/ppermute | solution.py:32
  513.5 4.5 collective-permute-start.64
  (683 shorter events, 341.4 us)
Async XLA Ops:
  0.7 60.7 %collective-permute-start.38 = (bf16[192,1024]{1,0:T(8,128)(2,1)}, bf16[192,1024]{1,0:T(8,128)(2,1)S(1)}, u32[]{:S(2)}, u32[]{:S(2)}) collective-permute-start(bf16[192,1024]{1,0:T(8,128)(2,1)} %bitcast.726), channel_id=1, source_target_pairs={{0,32},{8,40},{16,48},{24,56},{32,64},{40,72},{48,80},{56,88},{64,... | collective-permute-start | bytes 1179656 | tf_op jit(solution)/shard_map/ppermute | solution.py:25
  2.8 64.4 %collective-permute-start.39 = (bf16[192,1024]{1,0:T(8,128)(2,1)}, bf16[192,1024]{1,0:T(8,128)(2,1)S(1)}, u32[]{:S(2)}, u32[]{:S(2)}) collective-permute-start(bf16[192,1024]{1,0:T(8,128)(2,1)} %bitcast.727), channel_id=1, source_target_pairs={{0,64},{8,72},{16,80},{24,88},{32,96},{40,104},{48,112},{56,120},{... | collective-permute-start | bytes 1179656 | tf_op jit(solution)/shard_map/ppermute | solution.py:25
  5.2 61.9 %collective-permute-start.40 = (bf16[192,1024]{1,0:T(8,128)(2,1)}, bf16[192,1024]{1,0:T(8,128)(2,1)S(1)}, u32[]{:S(2)}, u32[]{:S(2)}) collective-permute-start(bf16[192,1024]{1,0:T(8,128)(2,1)} %bitcast.728), channel_id=1, source_target_pairs={{0,96},{8,104},{16,112},{24,120},{32,0},{40,8},{48,16},{56,24},{64... | collective-permute-start | bytes 1179656 | tf_op jit(solution)/shard_map/ppermute | solution.py:25
  12.2 27.4 %collective-permute-start.28 = (bf16[72,1024]{1,0:T(8,128)(2,1)}, bf16[72,1024]{1,0:T(8,128)(2,1)}, u32[]{:S(2)}, u32[]{:S(2)}) collective-permute-start(bf16[72,1024]{1,0:T(8,128)(2,1)} %constant_dynamic-slice_fusion), channel_id=1, source_target_pairs={{0,0},{1,8},{2,32},{3,40},{4,64},{5,72},{6,96},{7,104},{16,16},{17... | collective-permute-start | bytes 442376 | tf_op jit(solution)/shard_map/ppermute | solution.py:43
  57.4 29.0 %collective-permute-start.1 = (bf16[208,1024]{1,0:T(8,128)(2,1)S(1)}, bf16[208,1024]{1,0:T(8,128)(2,1)S(1)}, u32[]{:S(2)}, u32[]{:S(2)}) collective-permute-start(bf16[208,1024]{1,0:T(8,128)(2,1)S(1)} %fusion.69), channel_id=1, source_target_pairs={{0,32},{8,40},{16,48},{24,56},{32,64},{40,72},{48,80},{56,88},{64,... | collective-permute-start | bytes 1277960 | tf_op jit(solution)/shard_map/ppermute | solution.py:25
  61.3 29.0 %collective-permute-start.2 = (bf16[208,1024]{1,0:T(8,128)(2,1)S(1)}, bf16[208,1024]{1,0:T(8,128)(2,1)S(1)}, u32[]{:S(2)}, u32[]{:S(2)}) collective-permute-start(bf16[208,1024]{1,0:T(8,128)(2,1)S(1)} %fusion.69), channel_id=1, source_target_pairs={{0,64},{8,72},{16,80},{24,88},{32,96},{40,104},{48,112},{56,120},{... | collective-permute-start | bytes 1277960 | tf_op jit(solution)/shard_map/ppermute | solution.py:25
  67.2 54.7 %collective-permute-start.30 = (bf16[2,72,1024]{2,1,0:T(8,128)(2,1)}, bf16[2,72,1024]{2,1,0:T(8,128)(2,1)S(1)}, u32[]{:S(2)}, u32[]{:S(2)}) collective-permute-start(bf16[2,72,1024]{2,1,0:T(8,128)(2,1)} %pad_maximum_fusion.23), channel_id=1, source_target_pairs={{0,2},{1,3},{2,4},{3,5},{4,6},{5,7},{6,0},{7,1},{8,10},{9,11},{10,... | collective-permute-start | bytes 884744 | tf_op jit(solution)/shard_map/ppermute | solution.py:32
  69.2 52.9 %collective-permute-start.31 = (bf16[2,72,1024]{2,1,0:T(8,128)(2,1)}, bf16[2,72,1024]{2,1,0:T(8,128)(2,1)S(1)}, u32[]{:S(2)}, u32[]{:S(2)}) collective-permute-start(bf16[2,72,1024]{2,1,0:T(8,128)(2,1)} %pad_maximum_fusion.23), channel_id=1, source_target_pairs={{0,4},{1,5},{2,6},{3,7},{4,0},{5,1},{6,2},{7,3},{8,12},{9,13},{10,... | collective-permute-start | bytes 884744 | tf_op jit(solution)/shard_map/ppermute | solution.py:32
  86.4 30.8 %collective-permute-start.16 = (bf16[2,128,1280]{2,1,0:T(8,128)(2,1)S(1)}, bf16[2,128,1280]{2,1,0:T(8,128)(2,1)S(1)}, u32[]{:S(2)}, u32[]{:S(2)}) collective-permute-start(bf16[2,128,1280]{2,1,0:T(8,128)(2,1)S(1)} %pad_maximum_fusion.17), channel_id=1, source_target_pairs={{0,4},{1,5},{2,6},{3,7},{4,0},{5,1},{6,2},{7,3},{8,12},{9,13},{10,... | collective-permute-start | bytes 1966088 | tf_op jit(solution)/shard_map/ppermute | solution.py:32
  90.3 27.6 %collective-permute-start.17 = (bf16[2,128,1280]{2,1,0:T(8,128)(2,1)S(1)}, bf16[2,128,1280]{2,1,0:T(8,128)(2,1)S(1)}, u32[]{:S(2)}, u32[]{:S(2)}) collective-permute-start(bf16[2,128,1280]{2,1,0:T(8,128)(2,1)S(1)} %pad_maximum_fusion.17), channel_id=1, source_target_pairs={{0,6},{1,7},{2,0},{3,1},{4,2},{5,3},{6,4},{7,5},{8,14},{9,15},{10,... | collective-permute-start | bytes 1966088 | tf_op jit(solution)/shard_map/ppermute | solution.py:32
  102.5 33.8 %collective-permute-start.4 = (bf16[3,208,1024]{2,1,0:T(8,128)(2,1)S(1)}, bf16[3,208,1024]{2,1,0:T(8,128)(2,1)S(1)}, u32[]{:S(2)}, u32[]{:S(2)}) collective-permute-start(bf16[3,208,1024]{2,1,0:T(8,128)(2,1)S(1)} %pad_maximum_fusion.4), channel_id=1, source_target_pairs={{0,8},{8,0},{16,24},{24,16},{32,40},{40,32},{48,56},{56,48},{64,72... | collective-permute-start | bytes 3833864 | tf_op jit(solution)/shard_map/ppermute | solution.py:25
  125.5 81.6 %collective-permute-start.32 = (bf16[2,72,1024]{2,1,0:T(8,128)(2,1)}, bf16[2,72,1024]{2,1,0:T(8,128)(2,1)}, u32[]{:S(2)}, u32[]{:S(2)}) collective-permute-start(bf16[2,72,1024]{2,1,0:T(8,128)(2,1)} %pad_maximum_fusion.23), channel_id=1, source_target_pairs={{0,6},{1,7},{2,0},{3,1},{4,2},{5,3},{6,4},{7,5},{8,14},{9,15},{10,... | collective-permute-start | bytes 884744 | tf_op jit(solution)/shard_map/ppermute | solution.py:32
  132.3 76.5 %collective-permute-start.41 = (bf16[3,192,1024]{2,1,0:T(8,128)(2,1)}, bf16[3,192,1024]{2,1,0:T(8,128)(2,1)}, u32[]{:S(2)}, u32[]{:S(2)}) collective-permute-start(bf16[3,192,1024]{2,1,0:T(8,128)(2,1)} %pad_maximum_fusion.7), channel_id=1, source_target_pairs={{0,8},{8,0},{16,24},{24,16},{32,40},{40,32},{48,56},{56,48},{64,72... | collective-permute-start | bytes 3538952 | tf_op jit(solution)/shard_map/ppermute | solution.py:25
  135.7 30.5 %collective-permute-start.22 = (bf16[3,1024,128]{2,1,0:T(8,128)(2,1)}, bf16[3,1024,128]{2,1,0:T(8,128)(2,1)}, u32[]{:S(2)}, u32[]{:S(2)}) collective-permute-start(bf16[3,1024,128]{2,1,0:T(8,128)(2,1)} %pad_maximum_fusion.15), channel_id=1, source_target_pairs={{0,8},{8,0},{16,24},{24,16},{32,40},{40,32},{48,56},{56,48},{64,72... | collective-permute-start | bytes 2359304 | tf_op jit(solution)/shard_map/ppermute | solution.py:25
  263.8 57.5 %collective-permute-start.69 = (bf16[4,128,1152]{2,1,0:T(8,128)(2,1)S(1)}, bf16[4,128,1152]{2,1,0:T(8,128)(2,1)S(1)}, u32[]{:S(2)}, u32[]{:S(2)}) collective-permute-start(bf16[4,128,1152]{2,1,0:T(8,128)(2,1)S(1)} %fusion.9), channel_id=1, source_target_pairs={{0,1},{1,0},{2,3},{3,2},{4,5},{5,4},{6,7},{7,6},{8,9},{9,8},{10,11... | collective-permute-start | bytes 3538952 | tf_op jit(solution)/shard_map/ppermute | solution.py:32
  281.0 22.9 %collective-permute-start.83 = (bf16[72,1024]{1,0:T(8,128)(2,1)S(1)}, bf16[72,1024]{1,0:T(8,128)(2,1)S(1)}, u32[]{:S(2)}, u32[]{:S(2)}) collective-permute-start(bf16[72,1024]{1,0:T(8,128)(2,1)S(1)} %fusion.104), channel_id=1, source_target_pairs={{0,16},{8,24},{16,0},{24,8},{32,48},{40,56},{48,32},{56,40},{64,80... | collective-permute-start | bytes 442376 | tf_op jit(solution)/shard_map/ppermute | solution.py:25
  286.5 58.7 %collective-permute-start.33 = (bf16[4,192,1024]{2,1,0:T(8,128)(2,1)S(1)}, bf16[4,192,1024]{2,1,0:T(8,128)(2,1)S(1)}, u32[]{:S(2)}, u32[]{:S(2)}) collective-permute-start(bf16[4,192,1024]{2,1,0:T(8,128)(2,1)S(1)} %slice_bitcast_fusion.2), channel_id=1, source_target_pairs={{0,8},{8,0},{16,24},{24,16},{32,40},{40,32},{48,56},{56,48},{64,72... | collective-permute-start | bytes 4718600 | tf_op jit(solution)/shard_map/ppermute | solution.py:25
  307.8 38.0 %collective-permute-start.42 = (bf16[4,192,1024]{2,1,0:T(8,128)(2,1)S(1)}, bf16[4,192,1024]{2,1,0:T(8,128)(2,1)S(1)}, u32[]{:S(2)}, u32[]{:S(2)}) collective-permute-start(bf16[4,192,1024]{2,1,0:T(8,128)(2,1)S(1)} %slice_bitcast_fusion.1), channel_id=1, source_target_pairs={{0,8},{8,0},{16,24},{24,16},{32,40},{40,32},{48,56},{56,48},{64,72... | collective-permute-start | bytes 4718600 | tf_op jit(solution)/shard_map/ppermute | solution.py:25
  345.7 36.6 %collective-permute-start.34 = (bf16[192,1024]{1,0:T(8,128)(2,1)S(1)}, bf16[192,1024]{1,0:T(8,128)(2,1)S(1)}, u32[]{:S(2)}, u32[]{:S(2)}) collective-permute-start(bf16[192,1024]{1,0:T(8,128)(2,1)S(1)} %get-tuple-element.73), channel_id=1, source_target_pairs={{0,96},{8,104},{16,112},{24,120},{32,0},{40,8},{48,16},{56,24},{64... | collective-permute-start | bytes 1179656 | tf_op jit(solution)/shard_map/ppermute | solution.py:25
  345.8 40.9 %collective-permute-start.35 = (bf16[192,1024]{1,0:T(8,128)(2,1)S(1)}, bf16[192,1024]{1,0:T(8,128)(2,1)S(1)}, u32[]{:S(2)}, u32[]{:S(2)}) collective-permute-start(bf16[192,1024]{1,0:T(8,128)(2,1)S(1)} %get-tuple-element.75), channel_id=1, source_target_pairs={{0,64},{8,72},{16,80},{24,88},{32,96},{40,104},{48,112},{56,120},{... | collective-permute-start | bytes 1179656 | tf_op jit(solution)/shard_map/ppermute | solution.py:25
  346.3 26.1 %collective-permute-start.43 = (bf16[192,1024]{1,0:T(8,128)(2,1)S(1)}, bf16[192,1024]{1,0:T(8,128)(2,1)S(1)}, u32[]{:S(2)}, u32[]{:S(2)}) collective-permute-start(bf16[192,1024]{1,0:T(8,128)(2,1)S(1)} %get-tuple-element.70), channel_id=1, source_target_pairs={{0,96},{8,104},{16,112},{24,120},{32,0},{40,8},{48,16},{56,24},{64... | collective-permute-start | bytes 1179656 | tf_op jit(solution)/shard_map/ppermute | solution.py:25
  393.6 73.8 %collective-permute-start.55 = (bf16[4,1024,128]{2,1,0:T(8,128)(2,1)}, bf16[4,1024,128]{2,1,0:T(8,128)(2,1)}, u32[]{:S(2)}, u32[]{:S(2)}) collective-permute-start(bf16[4,1024,128]{2,1,0:T(8,128)(2,1)} %fusion.13), channel_id=1, source_target_pairs={{0,8},{8,0},{16,24},{24,16},{32,40},{40,32},{48,56},{56,48},{64,72... | collective-permute-start | bytes 3145736 | tf_op jit(solution)/shard_map/ppermute | solution.py:25
  400.8 63.8 %collective-permute-start.78 = (bf16[3,128,1152]{2,1,0:T(8,128)(2,1)}, bf16[3,128,1152]{2,1,0:T(8,128)(2,1)}, u32[]{:S(2)}, u32[]{:S(2)}) collective-permute-start(bf16[3,128,1152]{2,1,0:T(8,128)(2,1)} %pad_maximum_fusion.12), channel_id=1, source_target_pairs={{0,8},{8,0},{16,24},{24,16},{32,40},{40,32},{48,56},{56,48},{64,72... | collective-permute-start | bytes 2654216 | tf_op jit(solution)/shard_map/ppermute | solution.py:25
  463.3 62.0 %collective-permute-start.51 = (bf16[4,192,1024]{2,1,0:T(8,128)(2,1)S(1)}, bf16[4,192,1024]{2,1,0:T(8,128)(2,1)S(1)}, u32[]{:S(2)}, u32[]{:S(2)}) collective-permute-start(bf16[4,192,1024]{2,1,0:T(8,128)(2,1)S(1)} %slice_bitcast_fusion), channel_id=1, source_target_pairs={{0,8},{8,0},{16,24},{24,16},{32,40},{40,32},{48,56},{56,48},{64,72... | collective-permute-start | bytes 4718600 | tf_op jit(solution)/shard_map/ppermute | solution.py:25
  (158 other events, 1624.7 us)
